TPU v7x, 32 devices: a whole 2x2x4 slice. The times are simulated.
32 devices in a mesh: groups: 2 (over x), span: 16 (over z, y, core).
Axes of the slice: x: 2, y: 2, z: 4, core: 2. Of those that a mesh axis runs over, the one named last changes fastest.
Arguments:
- hidden_in: bfloat16 [16384, 2240], P(('groups', 'span')), parts along dimension 0, may hold values from -16 to 16
- noisy_latents: float32 [16384, 32], P(('groups', 'span')), parts along dimension 0, may hold values from -6 to 6
- span_ids: int32 [16384], P(('groups', 'span')), parts along dimension 0, may hold values from 0 to 31, as said below
- tile_map: int32 [16384], P('groups'), parts along dimension 0, may hold values from 0 to 8191, as said below
- qkv_weight: bfloat16 [2240, 3360], replicated, may hold values from -0.125 to 0.125
- out_weight: bfloat16 [1120, 2240], replicated, may hold values from -0.1875 to 0.1875
- norm_gain: float32 [2240], replicated, may hold values from 0.1 to 1.9
- velocity_weight: bfloat16 [2240, 32], replicated, may hold values from -0.125 to 0.125
- conv_first: bfloat16 [3, 3, 32, 256], replicated, may hold values from -0.375 to 0.375
- conv_second: bfloat16 [3, 3, 256, 256], replicated, may hold values from -0.125 to 0.125
Outputs:
- new_latents: float32 [16384, 32], P(('groups', 'span')), parts along dimension 0
- decoded: bfloat16 [256, 64, 256], P(('groups', 'span')), parts along dimension 0
There are 2 independent parts, one for each index of `groups`. A program takes and returns all parts, laid end to end along the dimension named above; an argument that names none is the same for every part. Nothing has to cross between parts.
Inputs may be any that keep to these rules, and one draw needn't show every extreme that they name: `span_ids`: never falling along the tokens; every span number occurs, each span holds 1 to 1024 tokens, and one span holds exactly 1024. `tile_map`: A permutation of the 8192 grid positions; the 512 tokens of each aligned block of tokens place exactly 32 tokens in each aligned block of 512 positions.
All inputs are finite; a program needn't handle non-finite values.
Results may differ from a plain program's by a relative error of at most 0.01.
Values may be sent and summed in bfloat16 or wider, within the bound.
A program may use at most 128 MiB of HBM per device.

v0:
```python
import functools

import jax
import jax.numpy as jnp
from jax import lax
from jax.experimental import pallas as pl
from jax.experimental.pallas import tpu as pltpu
from jax.sharding import PartitionSpec as P

HDIM = 32
IW = 64
BLK = 256
BF = jnp.bfloat16
F32 = jnp.float32


def dot(a, b):
    return jnp.dot(a, b, preferred_element_type=F32)


def dot_nt(a, b):
    return lax.dot_general(a, b, (((1,), (1,)), ((), ())), preferred_element_type=F32)


def dot_tn(a, b):
    return lax.dot_general(a, b, (((0,), (0,)), ((), ())), preferred_element_type=F32)


def iota(shape, axis):
    return lax.broadcasted_iota(jnp.int32, shape, axis)


def kernel(
    cfg,
    hid_hbm, noisy, span_ref, map_ref, wq_hbm, wo_hbm, gain, vw, w1, w2_hbm,
    lat_out, dec_out,
    hidt, hid, wq, wo, w2, packed, qs, ks, vs, num, kvis, att,
    st_c0, st_b0, st_send, lead_send, pair_recv, lead_recv, half_send, half_recv,
    fin_send, fin_recv, carry, after, onehot, xlat, outgoing, incoming,
    wide, halo_send, halo_recv, first, shifted,
    wsem, lsem, psem, hsend, hrecv, fsem, lead_ssem, lead_rsem, asend, arecv, halo_ssem, halo_rsem,
):
    n, toks, d, inner, pad = cfg
    half = pad // 2
    chips = n // 2
    groups = pad // BLK
    me = lax.axis_index("span")
    core = lax.rem(me, 2)
    chip = me // 2
    partner = me + 1 - 2 * core
    share = toks // n
    chunk = toks // 2

    def remote(src, dst, ss, rs, dev):
        return pltpu.make_async_remote_copy(
            src_ref=src, dst_ref=dst, send_sem=ss, recv_sem=rs,
            device_id={"span": dev}, device_id_type=pl.DeviceIdType.MESH,
        )

    barrier = pltpu.get_barrier_semaphore()
    for k in range(1, n):
        pl.semaphore_signal(
            barrier, inc=1, device_id={"span": lax.rem(me + k, n)},
            device_id_type=pl.DeviceIdType.MESH,
        )

    total = wq_hbm.shape[1]
    full = total // BLK
    rest = total - full * BLK
    lo = inner // BLK

    def wcopy(b):
        cols = pl.ds(pl.multiple_of(b * BLK, BLK), BLK)
        return pltpu.make_async_copy(wq_hbm.at[:, cols], wq.at[:, cols], wsem.at[b])

    hcopy = pltpu.make_async_copy(hid_hbm, hidt, lsem.at[0])
    hcopy.start()
    for b in range(lo, full):
        wcopy(b).start()
    tail_copy = None
    if rest:
        tail_copy = pltpu.make_async_copy(
            wq_hbm.at[:, full * BLK : total], wq.at[:, full * BLK : total], wsem.at[full]
        )
        tail_copy.start()
    for b in range(lo):
        wcopy(b).start()
    ocopy = pltpu.make_async_copy(wo_hbm, wo, lsem.at[1])
    ocopy.start()
    w2copy = pltpu.make_async_copy(w2_hbm, w2, lsem.at[2])
    w2copy.start()

    span_row = span_ref[...].astype(F32)
    span_col = jnp.transpose(jnp.broadcast_to(span_row, (128, toks)))[:, 0:1]
    first_seg = span_col[0:1, :]
    last_seg = span_col[toks - 1 : toks, :]
    lasts = [span_col[(c + 1) * chunk - 1 : (c + 1) * chunk, :] for c in range(2)]

    hcopy.wait()

    def turn(i, c):
        cols = pl.ds(pl.multiple_of(i * 128, 128), 128)
        hid[cols, :] = jnp.transpose(hidt[:, cols])
        return c

    lax.fori_loop(0, toks // 128, turn, 0)

    def project(b, carry_in):
        wcopy(b).wait()
        cols = pl.ds(pl.multiple_of(b * BLK, BLK), BLK)
        packed[:, cols] = dot(hid[...], wq[:, cols]).astype(BF)
        return carry_in

    lax.fori_loop(lo, full, project, 0)
    if rest:
        tail_copy.wait()
        packed[:, full * BLK : total] = dot(hid[...], wq[:, full * BLK : total]).astype(BF)

    def shift_in(dst, begin, relu):
        base = begin // 128 * 128
        off = begin - base
        width = packed.shape[1]
        end = min(base + pad + 128, width)

        def rows(r, c):
            rs = pl.ds(pl.multiple_of(r * 128, 128), 128)
            val = packed[rs, base:end].astype(F32)
            if off:
                val = pltpu.roll(val, val.shape[1] - off, 1)
            val = val[:, :pad]
            if relu:
                val = jnp.maximum(val, 0.0)
            val = jnp.where(iota((128, pad), 1) < inner, val, 0.0)
            dst[rs, :] = val.astype(BF)
            return c

        lax.fori_loop(0, toks // 128, rows, 0)

    shift_in(ks, inner, True)
    shift_in(vs, 2 * inner, False)

    block = (iota((BLK, BLK), 0) // HDIM == iota((BLK, BLK), 1) // HDIM)
    block_f = block.astype(F32)

    def compact(full_state):
        kept = jnp.where(block, full_state, 0.0)
        out = kept[0:HDIM]
        for h in range(1, BLK // HDIM):
            out = out + kept[h * HDIM : (h + 1) * HDIM]
        return out

    def expand(small):
        return (jnp.concatenate([small] * (BLK // HDIM), axis=0) * block_f).astype(BF)

    lead_col = (span_col == first_seg).astype(F32)
    to_b0 = (span_col[chunk:, :] <= lasts[0]).astype(F32)

    def states(g, c):
        cols = pl.ds(pl.multiple_of(g * BLK, BLK), BLK)
        k8 = ks[:, cols]
        v8 = vs[:, cols]
        s0 = compact(dot_tn(k8[:chunk], v8[:chunk]))
        s1 = compact(dot_tn(k8[chunk:], v8[chunk:]))
        k1 = (k8[chunk:].astype(F32) * to_b0).astype(BF)
        sb = compact(dot_tn(k1, v8[chunk:]))
        kl = (k8.astype(F32) * lead_col).astype(BF)
        sl = compact(dot_tn(kl, v8))
        st_c0[:, cols] = s0
        st_b0[:, cols] = s0 + sb
        num[0:HDIM, cols] = s0 + s1
        num[HDIM : 2 * HDIM, cols] = sl
        return c

    lax.fori_loop(0, groups, states, 0)

    def pack_sums(dst, column):
        kf = ks[...].astype(F32)
        if column is not None:
            kf = kf * column
        sums = jnp.sum(kf, axis=0, keepdims=True)
        parts = [sums[:, 128 * r : 128 * (r + 1)] for r in range((inner + 127) // 128)]
        base_rows = jnp.zeros((HDIM, 128), F32)
        row_no = iota((HDIM, 128), 0)
        for r, part in enumerate(parts):
            base_rows = jnp.where(row_no == r, jnp.broadcast_to(part, (HDIM, 128)), base_rows)
        base_rows = jnp.where(
            row_no == HDIM - 1, jnp.broadcast_to(first_seg, (HDIM, 128)), base_rows
        )
        dst[:, pad - 128 :] = base_rows.astype(BF)

    st_send[:, : pad - 128] = num[0:HDIM, : pad - 128].astype(BF)
    lead_send[:, : pad - 128] = num[HDIM : 2 * HDIM, : pad - 128].astype(BF)
    pack_sums(st_send, None)
    pack_sums(lead_send, lead_col)

    pl.semaphore_wait(barrier, n - 1)
    pair = remote(st_send, pair_recv, psem.at[0], psem.at[1], partner)
    pair.start()

    def lead_copy(k):
        return remote(
            lead_send, lead_recv.at[k], lead_ssem.at[k], lead_rsem.at[k],
            lax.rem(me - 1 - k + n, n),
        )

    for k in range(2):

        @pl.when(me >= k + 1)
        def _(k=k):
            lead_copy(k).start()

    mine = map_ref[:, pl.ds(pl.multiple_of(me * toks, toks), toks)]
    target = mine // toks
    within = mine - target * toks
    hits = (iota((n, toks), 0) == jnp.broadcast_to(target, (n, toks))).astype(F32)
    upper = (iota((toks, toks), 0) <= iota((toks, toks), 1)).astype(BF)
    cum = dot(hits.astype(BF), upper)
    rank = jnp.sum(cum * hits, axis=0, keepdims=True).astype(jnp.int32) - 1
    slot = target * share + rank
    onehot[...] = (iota((toks, toks), 0) == jnp.broadcast_to(slot, (toks, toks))).astype(F32).astype(BF)
    line = (within // IW).astype(F32)
    spot = (within - within // IW * IW).astype(F32)
    row_no = iota((128, toks), 0)
    places = jnp.where(row_no == HDIM, jnp.broadcast_to(spot, (128, toks)), 0.0)
    places = jnp.where(row_no == HDIM + 1, jnp.broadcast_to(line, (128, toks)), places)
    xlat[...] = places

    pair.wait()
    lanes = pl.ds(pl.multiple_of(core * half, 128), half)
    half_send[...] = (st_send[:, lanes].astype(F32) + pair_recv[:, lanes].astype(F32)).astype(BF)

    def chip_copy(to):
        return remote(
            half_send, half_recv.at[chip], hsend.at[to], hrecv.at[chip], 2 * to + core
        )

    for to in range(1, chips):

        @pl.when(chip < to)
        def _(to=to):
            chip_copy(to).start()

    lax.fori_loop(0, lo, project, 0)
    shift_in(qs, 0, True)

    heads_per = BLK // HDIM
    lane_head = iota((1, BLK), 1) // HDIM
    masks = []
    for c in range(2):
        sc = span_col[c * chunk : (c + 1) * chunk, :]
        sr = span_row[:, c * chunk : (c + 1) * chunk]
        keep = (sr <= sc) & (sc < lasts[c])
        masks.append(keep.astype(F32))
    allowed = (span_row <= span_col).astype(F32).astype(BF)

    def local(g, heads):
        cols = pl.ds(g * BLK if isinstance(g, int) else pl.multiple_of(g * BLK, BLK), BLK)
        kvis[:, cols] = dot(allowed, ks[:, cols])
        for c in range(2):
            rs = pl.ds(c * chunk, chunk)
            q8 = qs[rs, cols]
            k8 = ks[rs, cols]
            v8 = vs[rs, cols]
            acc = None
            for h0 in range(0, heads, 2):
                parts = []
                vals = []
                for h in range(h0, min(h0 + 2, heads)):
                    hm = (lane_head == h).astype(F32).astype(BF)
                    parts.append((dot_nt(q8 * hm, k8) * masks[c]).astype(BF))
                    vals.append(v8 * hm)
                one = dot(jnp.concatenate(parts, axis=1), jnp.concatenate(vals, axis=0))
                acc = one if acc is None else acc + one
            num[rs, cols] = acc

    whole = inner // BLK

    def local_loop(g, carry_in):
        local(g, heads_per)
        return carry_in

    lax.fori_loop(0, whole, local_loop, 0)
    if inner > whole * BLK:
        local(whole, (inner - whole * BLK) // HDIM)

    fin_send[...] = jnp.zeros_like(fin_send)
    carry[:, lanes] = jnp.zeros((HDIM, half), F32)
    for src in range(chips - 1):

        @pl.when(src < chip)
        def _(src=src):
            remote(
                half_send, half_recv.at[src], hsend.at[src], hrecv.at[src], partner
            ).wait_recv()
            carry[:, lanes] = carry[:, lanes] + half_recv[src].astype(F32)

    fin_send[...] = carry[:, lanes].astype(BF)
    fin = remote(fin_send, fin_recv, fsem.at[0], fsem.at[1], partner)
    fin.start()
    after[...] = jnp.zeros_like(after)
    for k in range(2):

        @pl.when(me + 1 + k < n)
        def _(k=k):
            remote(
                lead_send, lead_recv.at[k], lead_ssem.at[k], lead_rsem.at[k], partner
            ).wait_recv()
            got = lead_recv[k].astype(F32)
            same = (got[HDIM - 1 : HDIM, pad - 128 : pad - 127] == last_seg).astype(F32)
            after[...] = after[...] + got * same

    fin.wait()
    other = pl.ds(pl.multiple_of((1 - core) * half, 128), half)
    carry[:, other] = fin_recv[...].astype(F32)

    @pl.when(core == 1)
    def _():
        carry[...] = carry[...] + pair_recv[...].astype(F32)

    reach = [(lasts[c] == last_seg).astype(F32) for c in range(2)]
    dev_tail = (span_col == last_seg).astype(F32)
    tails = [
        (span_col[c * chunk : (c + 1) * chunk, :] == lasts[c]).astype(F32) for c in range(2)
    ]
    ones_block = block_f.astype(BF)

    def spread(ref, g):
        per = BLK // 128
        rows = [ref[pl.ds(per * g + r, 1), pad - 128 :] for r in range(per)]
        return jnp.concatenate(rows, axis=1)

    for g in range(groups):
        cols = pl.ds(g * BLK, BLK)
        valid = iota((1, BLK), 1) + g * BLK < inner
        live = (iota((HDIM, BLK), 1) + g * BLK) < inner
        zero = jnp.zeros((HDIM, BLK), F32)
        car = jnp.where(live, carry[:, cols], zero)
        aft = jnp.where(live, after[:, cols], zero)
        if g * BLK + BLK <= (inner + 127) // 128 * 128:
            csum, asum = spread(carry, g), spread(after, g)
        else:
            need = (inner - g * BLK + 127) // 128
            csum = jnp.concatenate(
                [carry[2 * g + r : 2 * g + r + 1, pad - 128 :] if r < need
                 else jnp.zeros((1, 128), F32) for r in range(2)], axis=1)
            asum = jnp.concatenate(
                [after[2 * g + r : 2 * g + r + 1, pad - 128 :] if r < need
                 else jnp.zeros((1, 128), F32) for r in range(2)], axis=1)
        csum = jnp.where(valid, csum, 0.0)
        asum = jnp.where(valid, asum, 0.0)
        st_all = jnp.where(live, st_send[:, cols].astype(F32), zero)
        for c in range(2):
            rs = pl.ds(c * chunk, chunk)
            q8 = qs[rs, cols].astype(F32)
            q_tail = (q8 * tails[c]).astype(BF)
            q_non = (q8 * (1.0 - tails[c])).astype(BF)
            if c == 0:
                a_state = car
                b_state = st_b0[:, cols] + car + aft * reach[0]
            else:
                a_state = st_c0[:, cols] + car
                b_state = st_all + car + aft
            numer = num[rs, cols] + dot(q_non, expand(a_state)) + dot(q_tail, expand(b_state))
            seen = kvis[rs, cols] + csum + dev_tail[c * chunk : (c + 1) * chunk] * asum
            den = dot((q8 * seen).astype(BF), ones_block)
            att[rs, cols] = (numer / (1.0 + den)).astype(BF)

    ocopy.wait()

    def tail_rows(r, c):
        rs = pl.ds(pl.multiple_of(r * BLK, BLK), BLK)
        mixed = hid[rs, :].astype(F32) + dot(att[rs, :inner], wo[...])
        meansq = jnp.sum(mixed * mixed, axis=1, keepdims=True) * (1.0 / d)
        normed = (mixed * lax.rsqrt(meansq + 1e-06) * jnp.broadcast_to(gain[...][None, :], (BLK, d))).astype(BF)
        lat = noisy[:, rs] - 0.5 * dot_nt(vw[...], normed)
        lat_out[:, rs] = lat
        xlat[0:HDIM, rs] = lat
        return c

    lax.fori_loop(0, toks // BLK, tail_rows, 0)

    outgoing[...] = dot_nt(onehot[...], xlat[...].astype(BF)).astype(BF)

    def out_copy(k):
        to = lax.rem(me + k, n)
        return remote(
            outgoing.at[pl.ds(pl.multiple_of(to * share, share), share)],
            incoming.at[pl.ds(pl.multiple_of(me * share, share), share)],
            asend.at[k], arecv.at[me], to,
        )

    for k in range(1, n):
        out_copy(k).start()
    own = pl.ds(pl.multiple_of(me * share, share), share)
    incoming[own, :] = outgoing[own, :]
    for k in range(1, n):
        src = lax.rem(me + k, n)
        remote(
            outgoing.at[pl.ds(0, share)],
            incoming.at[pl.ds(pl.multiple_of(src * share, share), share)],
            asend.at[k], arecv.at[src], src,
        ).wait_recv()

    got = incoming[...]
    lane_no = iota((8, 128), 1)
    pick = jnp.where(lane_no == HDIM, 1.0, jnp.where(lane_no == HDIM + 1, float(IW), 0.0)).astype(BF)
    pos = dot_nt(pick, got)[0:1, :].astype(jnp.int32)
    onehot[...] = (iota((toks, toks), 0) == jnp.broadcast_to(pos, (toks, toks))).astype(F32).astype(BF)
    tile = dot(onehot[...], got)
    edge = 2 * IW
    wide[edge : edge + toks, :] = tile
    halo_send[0] = tile[:edge].astype(BF)
    halo_send[1] = tile[toks - edge :].astype(BF)

    def halo(k, to):
        return remote(halo_send.at[k], halo_recv.at[k], halo_ssem.at[k], halo_rsem.at[k], to)

    @pl.when(me > 0)
    def _():
        halo(0, me - 1).start()

    @pl.when(me < n - 1)
    def _():
        halo(1, me + 1).start()

    wide[0:edge, :] = jnp.zeros((edge, 128), F32)
    wide[edge + toks :, :] = jnp.zeros((edge, 128), F32)

    @pl.when(me > 0)
    def _():
        halo(1, partner).wait_recv()
        wide[0:edge, :] = halo_recv[1].astype(F32)

    @pl.when(me < n - 1)
    def _():
        halo(0, partner).wait_recv()
        wide[edge + toks :, :] = halo_recv[0].astype(F32)

    ext = toks + 2 * edge
    x = wide[...]
    column = lax.rem(iota((ext, 128), 0), IW)
    lane = iota((ext, 128), 1)
    left = jnp.where(column == 0, 0.0, pltpu.roll(x, 1, 0))
    right = jnp.where(column == IW - 1, 0.0, pltpu.roll(x, ext - 1, 0))
    three = jnp.where(
        lane < HDIM, left,
        jnp.where(lane < 2 * HDIM, pltpu.roll(x, HDIM, 1),
                  jnp.where(lane < 3 * HDIM, pltpu.roll(right, 2 * HDIM, 1), 0.0)),
    )
    three = three.astype(BF)
    mid = toks + 2 * IW
    k3 = 3 * HDIM
    acc = dot(three[0:mid, :k3], w1[0])
    acc = acc + dot(three[IW : IW + mid, :k3], w1[1])
    acc = acc + dot(three[2 * IW : 2 * IW + mid, :k3], w1[2])
    feat = acc / (1.0 + jnp.exp(-acc))
    row_at = iota((mid, 1), 0) // IW
    outside = ((row_at == 0) & (me == 0)) | ((row_at == mid // IW - 1) & (me == n - 1))
    feat = jnp.where(outside, 0.0, feat).astype(BF).astype(F32)
    column = lax.rem(iota((mid, 1), 0), IW)
    shifted[1] = feat.astype(BF)
    shifted[0] = jnp.where(column == 0, 0.0, pltpu.roll(feat, 1, 0)).astype(BF)
    shifted[2] = jnp.where(column == IW - 1, 0.0, pltpu.roll(feat, mid - 1, 0)).astype(BF)
    w2copy.wait()
    out = None
    for a in range(3):
        for b in range(3):
            part = dot(shifted[b, a * IW : a * IW + toks, :], w2[3 * a + b])
            out = part if out is None else out + part
    dec_out[...] = out.astype(BF)

    for k in range(2):

        @pl.when(me >= k + 1)
        def _(k=k):
            lead_copy(k).wait_send()

    for to in range(1, chips):

        @pl.when(chip < to)
        def _(to=to):
            chip_copy(to).wait_send()

    for k in range(1, n):
        out_copy(k).wait_send()

    @pl.when(me > 0)
    def _():
        halo(0, me - 1).wait_send()

    @pl.when(me < n - 1)
    def _():
        halo(1, me + 1).wait_send()


def body(
    hidden_in, noisy_latents, span_ids, tile_map, qkv_weight, out_weight,
    norm_gain, velocity_weight, conv_first, conv_second,
):
    toks, d = hidden_in.shape
    inner = out_weight.shape[0]
    n = lax.axis_size("span")
    pad = -(-(inner + 128) // BLK) * BLK
    ch = conv_first.shape[3]
    wide_cols = -(-qkv_weight.shape[1] // 128) * 128
    pack_cols = max(wide_cols, 2 * inner // 128 * 128 + pad + 128)
    chips = n // 2
    edge = 2 * IW
    mid = toks + 2 * IW
    blocks = -(-qkv_weight.shape[1] // BLK)
    vm, dma = pltpu.VMEM, pltpu.SemaphoreType.DMA
    any_, vmem = pl.BlockSpec(memory_space=pl.ANY), pl.BlockSpec(memory_space=pltpu.VMEM)
    scratch = [
        vm((d, toks), BF), vm((toks, d), BF), vm(qkv_weight.shape, BF), vm(out_weight.shape, BF),
        vm((9, ch, ch), BF), vm((toks, pack_cols), BF),
        vm((toks, pad), BF), vm((toks, pad), BF), vm((toks, pad), BF),
        vm((toks, pad), F32), vm((toks, pad), F32), vm((toks, pad), BF),
        vm((HDIM, pad), F32), vm((HDIM, pad), F32),
        vm((HDIM, pad), BF), vm((HDIM, pad), BF), vm((HDIM, pad), BF), vm((2, HDIM, pad), BF),
        vm((HDIM, pad // 2), BF), vm((chips, HDIM, pad // 2), BF),
        vm((HDIM, pad // 2), BF), vm((HDIM, pad // 2), BF),
        vm((HDIM, pad), F32), vm((HDIM, pad), F32),
        vm((toks, toks), BF), vm((128, toks), F32),
        vm((toks, 128), BF), vm((toks, 128), BF),
        vm((toks + 2 * edge, 128), F32), vm((2, edge, 128), BF), vm((2, edge, 128), BF),
        vm((8, 128), BF), vm((3, mid, ch), BF),
        dma((blocks,)), dma((3,)), dma((2,)), dma((chips,)), dma((chips,)), dma((2,)),
        dma((2,)), dma((2,)), dma((n,)), dma((n,)), dma((2,)), dma((2,)),
    ]
    latents, decoded = pl.pallas_call(
        functools.partial(kernel, (n, toks, d, inner, pad)),
        out_shape=(
            jax.ShapeDtypeStruct(noisy_latents.shape[::-1], F32),
            jax.ShapeDtypeStruct((toks, ch), BF),
        ),
        in_specs=[any_, vmem, vmem, vmem, any_, any_, vmem, vmem, vmem, any_],
        out_specs=(vmem, vmem),
        scratch_shapes=scratch,
        compiler_params=pltpu.CompilerParams(
            collective_id=0, has_side_effects=True, vmem_limit_bytes=60 * 1024 * 1024
        ),
    )(
        hidden_in.T, noisy_latents.T, span_ids.reshape(1, toks), tile_map.reshape(1, -1),
        qkv_weight, out_weight, norm_gain, velocity_weight.T,
        conv_first.reshape(3, 3 * HDIM, ch), conv_second.reshape(9, ch, ch),
    )
    return latents.T, decoded.reshape(toks // IW, IW, ch)


def solution(mesh):
    rows = P(("groups", "span"), None)
    placed = (rows, rows, P(("groups", "span")), P("groups")) + (P(),) * 6
    return jax.shard_map(
        body, mesh=mesh, in_specs=placed,
        out_specs=(rows, P(("groups", "span"), None, None)), check_vma=False,
    )
```

profile of v0, /device:TPU:1, one launch (start us, length us, event | category | flops | bytes accessed | tf_op | source)
XLA Modules:
  0.0 58.5 jit_solution(18385885964495303927)
XLA Ops:
  0.6 54.7 %shard_map.113 = (f32[32,512]{1,0:T(8,128)}, bf16[512,256]{1,0:T(8,128)(2,1)}) custom-call(bf16[2240,512]{1,0:T(8,128)(2,1)} %bitcast.9, f32[32,512]{1,0:T(8,128)} %bitcast.14, s32[1,512]{1,0:T(1,128)} %bitcast.17, s32[1,8192]{1,0:T(1,128)} %bitcast.16, bf16[2240,3360]{1,0:T(8,128)(2,1)} %wq_hbm.1, bf16[1120,2240]{1,0:T(8,128)(2,1)} %wo_hbm.1, f32[2240]{0:T(1024)} %gain.1, ...), custom_call_target="tpu_custom_call" | custom-call | tf_op jit(solution)/shard_map/pallas_call | solution.py:530
  55.4 1.5 %copy.14 = f32[512,32]{0,1:T(8,128)} copy(f32[512,32]{0,1:T(8,128)} %bitcast.15) | data formatting | bytes 131072
  56.8 1.7 %copy.15 = bf16[8,64,256]{2,1,0:T(8,128)(2,1)} copy(bf16[8,64,256]{2,1,0:T(8,128)(2,1)} %bitcast.11) | data formatting | bytes 524288
where the time goes:
time: 58.7 us; the launch traced here: 58.5 us
  Pallas kernels  54.7 us (93%)
  local copies, waits for them, and re-layouts  3.14 us (5%)
  between operations  0.64 us (1%)
    pallas_call x1, Pallas kernels, body(): pl.pallas_call(functools.partial(kernel, (n, toks, d, inner, pad)), out_s...  54.7 us
    unnamed x2, local copies, waits for them, and re-layouts  3.14 us

commit v1 on v0

v1 whole, which is shorter than its diff:
```python
import functools

import jax
import jax.numpy as jnp
from jax import lax
from jax.experimental import pallas as pl
from jax.experimental.pallas import tpu as pltpu
from jax.sharding import PartitionSpec as P

HDIM = 32
IW = 64
BLK = 256
LANE = 128
PER = LANE // HDIM
TEAM = 4
LAG = 3
AHEAD = 4
BF = jnp.bfloat16
F32 = jnp.float32


def dot(a, b):
    return jnp.dot(a, b, preferred_element_type=F32)


def dot_nt(a, b):
    return lax.dot_general(a, b, (((1,), (1,)), ((), ())), preferred_element_type=F32)


def iota(shape, axis):
    return lax.broadcasted_iota(jnp.int32, shape, axis)


def kernel(
    cfg,
    hid_hbm, noisy_hbm, span_hbm, map_hbm, wq_hbm, wo_hbm, gain_hbm, vw_hbm, w1_hbm, w2_hbm,
    lat_out, dec_out,
    noisy, span_ref, map_ref, gain, vw, w1,
    hidt, hid, wq, wo, w2, qt, kp, vt, numt, dent, keep, att, ybuf, vwt, vel,
    st_c0, st_b0, sum_c0, sum_b0, st_send, lead_send, lead_recv,
    part_recv, plane_send, plane_recv, fin_send, fin_recv, base, carry, after, onehot, xlat, outgoing, incoming,
    wide, halo_send, halo_recv, shifted,
    wsem, lsem, hsem, isem, psend, precv, gsend, grecv, fsend, frecv, lead_ssem, lead_rsem, asend, arecv, halo_ssem, halo_rsem,
):
    n, toks, d, inner = cfg
    me = lax.axis_index("span")
    mate = lax.rem(me, TEAM)
    team = me // TEAM
    teams = n // TEAM
    share = toks // n
    chunk = toks // 2
    lo = inner // BLK
    koff = inner - lo * BLK
    kw = kp.shape[1]
    tiles = kw // LANE
    units = st_send.shape[0]
    part = units // TEAM
    heads = inner // HDIM
    first_slot = koff // HDIM
    last_slot = first_slot + heads

    def remote(src, dst, ss, rs, dev):
        return pltpu.make_async_remote_copy(
            src_ref=src, dst_ref=dst, send_sem=ss, recv_sem=rs,
            device_id={"span": dev}, device_id_type=pl.DeviceIdType.MESH,
        )

    total = wq_hbm.shape[1]
    full = total // BLK
    rest = total - full * BLK

    def wcopy(b):
        cols = slice(b * BLK, min(b * BLK + BLK, total))
        return pltpu.make_async_copy(wq_hbm.at[:, cols], wq.at[:, cols], wsem.at[b])

    def hcopy(i):
        cols = pl.ds(i * LANE if isinstance(i, int) else pl.multiple_of(i * LANE, LANE), LANE)
        return pltpu.make_async_copy(hid_hbm.at[:, cols], hidt.at[:, cols], hsem.at[i])

    for i in range(toks // LANE):
        hcopy(i).start()
    smalls = [
        pltpu.make_async_copy(src, dst, isem.at[i])
        for i, (src, dst) in enumerate([
            (span_hbm, span_ref), (vw_hbm, vw), (map_hbm, map_ref), (noisy_hbm, noisy),
            (gain_hbm, gain), (w1_hbm, w1),
        ])
    ]
    for copy in smalls[:2]:
        copy.start()
    ocopy = pltpu.make_async_copy(wo_hbm, wo.at[koff : koff + inner], lsem.at[1])
    w2copy = pltpu.make_async_copy(w2_hbm, w2, lsem.at[2])
    pending = [wcopy(full)] if rest else []
    pending += [wcopy(b) for b in range(lo, full)] + smalls[2:] + [wcopy(b) for b in range(lo)] + [ocopy, w2copy]

    def fetch(count):
        for copy in pending[:count]:
            copy.start()
        del pending[:count]

    fetch(AHEAD)

    barrier = pltpu.get_barrier_semaphore()
    for k in range(1, n):
        pl.semaphore_signal(
            barrier, inc=1, device_id={"span": lax.rem(me + k, n)},
            device_id_type=pl.DeviceIdType.MESH,
        )

    def clear(ref, row0, row1, dtype):
        if row1 > row0:
            ref[row0:row1, :] = jnp.zeros((row1 - row0, ref.shape[1]), dtype)

    for ref, dtype in ((qt, BF), (vt, BF), (numt, F32), (wo, BF)):
        clear(ref, 0, koff, dtype)
        clear(ref, koff + inner, kw, dtype)

    for j in (0, kw // BLK - 1):
        dent[j] = jnp.zeros((8, toks), F32)

    for copy in smalls[:2]:
        copy.wait()
    span_row = span_ref[...].astype(F32)
    span_col = jnp.transpose(jnp.broadcast_to(span_row, (LANE, toks)))[:, 0:1]
    first_seg = span_row[:, 0:1]
    last_seg = span_row[:, toks - 1 : toks]
    lasts = [span_row[:, (c + 1) * chunk - 1 : (c + 1) * chunk] for c in range(2)]
    for c in range(2):
        rs = slice(c * chunk, (c + 1) * chunk)
        sr = span_row[:, rs]
        keep[c] = ((span_col[rs, :] <= sr) & (sr < lasts[c])).astype(F32).astype(BF)
    vwt[...] = jnp.transpose(vw[...])

    def turn(i, c):
        cols = pl.ds(pl.multiple_of(i * LANE, LANE), LANE)
        hcopy(i).wait()
        hid[cols, :] = jnp.transpose(hidt[:, cols])
        return c

    lax.fori_loop(0, toks // LANE, turn, 0)
    fetch(2)

    if rest:
        wcopy(full).wait()
        tail_w = jnp.transpose(wq[:, full * BLK : total])
        row = full * BLK - 2 * inner + koff
        vt[row : row + rest, :] = dot(tail_w, hidt[...]).astype(BF)

    def finish(out, b, rs):
        begin, end = b * BLK, b * BLK + BLK
        if begin < 2 * inner:
            pos = jnp.maximum(out, jnp.zeros_like(out))
            if end > 2 * inner:
                pos = jnp.where(iota(out.shape, 1) < 2 * inner - begin, pos, out)
            out = pos
        if end > inner and begin < 2 * inner:
            kp[rs, begin - lo * BLK : end - lo * BLK] = out
        if begin < inner:
            rows = min(end, inner) - begin
            qt[koff + begin : koff + begin + rows, rs] = jnp.transpose(out)[:rows]
        if end > 2 * inner:
            skip = max(2 * inner - begin, 0)
            row = begin + skip - 2 * inner + koff
            vt[row : row + BLK - skip, rs] = jnp.transpose(out)[skip:]

    def project(blocks):
        for b in blocks:
            wcopy(b).wait()
        fetch(3)
        for at, b in enumerate(blocks):
            cols = slice(b * BLK, b * BLK + BLK)
            pair = len(blocks) % 2 == 1 and at == len(blocks) - 1
            for rs in [slice(0, chunk), slice(chunk, toks)] if pair else [slice(0, toks)]:
                finish(dot(hid[rs, :], wq[:, cols]).astype(BF), b, rs)

    early = list(range(lo, full))
    for at in range(0, len(early) - 1, 2):
        project(early[at : at + (2 if at + 3 < len(early) else 3)])
    for copy in smalls[2:]:
        copy.wait()

    ones16 = jnp.ones((16, chunk), F32).astype(BF)
    lead_row = (span_row == first_seg).astype(F32).astype(BF)
    b0_row = (span_row[:, chunk:] <= lasts[0]).astype(F32).astype(BF)
    lane_slot = iota((HDIM, LANE), 1) // HDIM

    def diag(res, t):
        parts = [res[(t * PER + i) * HDIM : (t * PER + i + 1) * HDIM, t * LANE : (t + 1) * LANE] for i in range(PER)]
        out = parts[PER - 1]
        for i in range(PER - 2, -1, -1):
            out = jnp.where(lane_slot == i, parts[i], out)
        return out

    for j in range(tiles // 2):
        cols = slice(j * BLK, (j + 1) * BLK)
        res = []
        for c in range(2):
            rs = slice(c * chunk, (c + 1) * chunk)
            k8 = kp[rs, cols]
            lhs = jnp.concatenate([vt[cols, rs], ones16], axis=0)
            res.append(dot(lhs, k8))
            res.append(dot(lhs * lead_row[:, rs], k8))
            if c == 1:
                res.append(dot(lhs * b0_row, k8))
        c0, l0, c1, l1, b0 = res
        for t in range(2):
            u = 2 * j + t
            s0 = diag(c0, t)
            st_c0[u] = s0
            st_b0[u] = s0 + diag(b0, t)
            st_send[u] = (s0 + diag(c1, t)).astype(BF)
            lead_send[u] = (diag(l0, t) + diag(l1, t)).astype(BF)
            at = slice(t * LANE, (t + 1) * LANE)
            one = slice(BLK, BLK + 1)
            sum_c0[0, u : u + 1, :] = c0[one, at]
            sum_b0[0, u : u + 1, :] = c0[one, at] + b0[one, at]
            sum_c0[1, u : u + 1, :] = c0[one, at] + c1[one, at]
            sum_b0[1, u : u + 1, :] = l0[one, at] + l1[one, at]

    half = HDIM // 2
    row_no = iota((half, LANE), 0)

    def pack_sums(dst, sums):
        sums = jnp.where(row_no < tiles, sums, 0.0)
        high = sums.astype(BF).astype(F32)
        low = sums - high
        high = jnp.where(row_no == half - 1, jnp.broadcast_to(first_seg, (half, LANE)), high)
        dst[tiles] = jnp.concatenate([high, low], axis=0).astype(BF)
        for u in range(tiles + 1, units):
            dst[u] = jnp.zeros((HDIM, LANE), F32).astype(BF)

    pack_sums(st_send, sum_c0[1])
    pack_sums(lead_send, sum_b0[1])

    pl.semaphore_wait(barrier, n - 1)

    def part_copy(k):
        to = lax.rem(mate + k, TEAM)
        return remote(
            st_send.at[pl.ds(part * to, part)], part_recv.at[mate],
            psend.at[k], precv.at[mate], team * TEAM + to,
        )

    for k in range(1, TEAM):
        part_copy(k).start()

    def lead_copy(k):
        return remote(
            lead_send, lead_recv.at[k], lead_ssem.at[k], lead_rsem.at[k],
            lax.rem(me - 1 - k + n, n),
        )

    for k in range(2):

        @pl.when(me >= k + 1)
        def _(k=k):
            lead_copy(k).start()

    mine = map_ref[:, pl.ds(pl.multiple_of(me * toks, toks), toks)]
    target = mine // toks
    within = mine - target * toks
    hits = (iota((n, toks), 0) == jnp.broadcast_to(target, (n, toks))).astype(F32)
    upper = (iota((toks, toks), 0) <= iota((toks, toks), 1)).astype(BF)
    cum = dot(hits.astype(BF), upper)
    rank = jnp.sum(cum * hits, axis=0, keepdims=True).astype(jnp.int32) - 1
    slot = target * share + rank
    onehot[...] = (iota((toks, toks), 0) == jnp.broadcast_to(slot, (toks, toks))).astype(F32).astype(BF)
    line = (within // IW).astype(F32)
    spot = (within - within // IW * IW).astype(F32)
    row_at = iota((128, toks), 0)
    places = jnp.where(row_at == HDIM, jnp.broadcast_to(spot, (128, toks)), 0.0)
    places = jnp.where(row_at == HDIM + 1, jnp.broadcast_to(line, (128, toks)), places)
    xlat[...] = places

    part_recv[mate] = st_send[pl.ds(part * mate, part)]
    for k in range(1, TEAM):
        src = lax.rem(mate + k, TEAM)
        remote(
            st_send.at[pl.ds(0, part)], part_recv.at[src], psend.at[k], precv.at[src], team * TEAM + src
        ).wait_recv()
    whole = part_recv[0].astype(F32)
    for src in range(1, TEAM):
        whole = whole + part_recv[src].astype(F32)
    plane_send[...] = whole.astype(BF)

    def plane_copy(to):
        return remote(
            plane_send, plane_recv.at[team], gsend.at[to], grecv.at[team], TEAM * to + mate
        )

    for to in range(1, teams):

        @pl.when(team < to)
        def _(to=to):
            plane_copy(to).start()

    fetch(len(pending))
    project(list(range(lo)))

    def attend(jobs):
        def place(j, s):
            t, i = s // PER, s % PER
            if isinstance(j, int):
                return pl.ds(j * BLK + s * HDIM, HDIM), pl.ds(j * BLK + t * LANE, LANE), i
            return (
                pl.ds(pl.multiple_of(j * BLK + s * HDIM, HDIM), HDIM),
                pl.ds(pl.multiple_of(j * BLK + t * LANE, LANE), LANE), i,
            )

        def scores(j, s, c):
            rs = slice(c * chunk, (c + 1) * chunk)
            head, tile, i = place(j, s)
            pieces = [qt[head, rs]]
            if i:
                pieces = [jnp.zeros((i * HDIM, chunk), BF)] + pieces
            if i < PER - 1:
                pieces = pieces + [jnp.zeros(((PER - 1 - i) * HDIM, chunk), BF)]
            return dot(kp[rs, tile], jnp.concatenate(pieces, axis=0)).astype(BF) * keep[c]

        def values(j, s, c, score):
            rs = slice(c * chunk, (c + 1) * chunk)
            head, _, _ = place(j, s)
            out = dot(jnp.concatenate([vt[head, rs], ones16], axis=0), score)
            numt[head, rs] = out[:HDIM]
            dent[j, s : s + 1, rs] = out[HDIM : HDIM + 1]

        queue = []
        for job in jobs:
            queue.append((job, scores(*job)))
            if len(queue) > LAG:
                old, score = queue.pop(0)
                values(*old, score)
        for old, score in queue:
            values(*old, score)

    slots_of = BLK // HDIM
    groups = kw // BLK
    plain, extra = [], []
    for j in range(groups):
        slots = [s for s in range(slots_of) if first_slot <= j * slots_of + s < last_slot]
        if len(slots) == slots_of:
            plain.append(j)
        else:
            extra += [(j, s, c) for s in slots for c in range(2)]
    attend(extra)

    def attend_loop(j, carry_in):
        attend([(j, s, c) for s in range(slots_of) for c in range(2)])
        return carry_in

    lax.fori_loop(plain[0], plain[-1] + 1, attend_loop, 0)

    base[...] = jnp.zeros_like(base)
    for src in range(teams - 1):

        @pl.when(src < team)
        def _(src=src):
            remote(
                plane_send, plane_recv.at[src], gsend.at[src], grecv.at[src], TEAM * src + mate
            ).wait_recv()
            base[...] = base[...] + plane_recv[src].astype(F32)

    run = base[...]
    for m in range(TEAM):
        fin_send[m] = run.astype(BF)
        if m < TEAM - 1:
            run = run + part_recv[m].astype(F32)

    def fin_copy(k):
        to = lax.rem(mate + k, TEAM)
        return remote(
            fin_send.at[to], fin_recv.at[mate], fsend.at[k], frecv.at[mate], team * TEAM + to
        )

    for k in range(1, TEAM):
        fin_copy(k).start()

    after[...] = jnp.zeros_like(after)
    for k in range(2):

        @pl.when(me + 1 + k < n)
        def _(k=k):
            remote(
                lead_send, lead_recv.at[k], lead_ssem.at[k], lead_rsem.at[k], lax.rem(me + 1 + k, n)
            ).wait_recv()
            same = (lead_recv[k, tiles, half - 1 : half, 0:1].astype(F32) == last_seg).astype(F32)
            after[...] = after[...] + lead_recv[k].astype(F32) * same

    fin_recv[mate] = fin_send[mate]
    for k in range(1, TEAM):
        src = lax.rem(mate + k, TEAM)
        remote(
            fin_send.at[0], fin_recv.at[src], fsend.at[k], frecv.at[src], team * TEAM + src
        ).wait_recv()
    for m in range(TEAM):
        carry[m * part : (m + 1) * part] = fin_recv[m].astype(F32)

    reach = [(lasts[c] == last_seg).astype(F32) for c in range(2)]
    tails = [span_row[:, c * chunk : (c + 1) * chunk] == lasts[c] for c in range(2)]
    masks = [(lane_slot == i).astype(F32).astype(BF) for i in range(PER)]
    den_slot = iota((half, LANE), 0)
    den_lane = iota((half, LANE), 1) // HDIM
    den_live = lax.rem(den_slot, PER) == den_lane

    def sums_of(ref, u):
        return ref[tiles, pl.ds(u, 1), :] + ref[tiles, pl.ds(half + u, 1), :]

    def combine(j, carry_in):
        packs = [[], []]
        for t in range(2):
            u = 2 * j + t
            tile = pl.ds(pl.multiple_of(j * BLK + t * LANE, LANE), LANE)
            car, aft = carry[u], after[u]
            csum, asum = sums_of(carry, u), sums_of(after, u)
            for c in range(2):
                rs = slice(c * chunk, (c + 1) * chunk)
                if c == 0:
                    a_state, a_sum = car, csum
                    b_state = st_b0[u] + car + aft * reach[0]
                    b_sum = sum_b0[0, pl.ds(u, 1), :] + csum + asum * reach[0]
                else:
                    a_state, a_sum = st_c0[u] + car, sum_c0[0, pl.ds(u, 1), :] + csum
                    b_state = st_send[u].astype(F32) + car + aft
                    b_sum = sum_c0[1, pl.ds(u, 1), :] + csum + asum
                a16, b16 = a_state.astype(BF), b_state.astype(BF)
                dens = []
                for s in (a_sum, b_sum):
                    high = s.astype(BF).astype(F32)
                    dens.append((high, s - high))
                (ah, al), (bh, bl) = dens
                den = jnp.where(den_slot < PER, ah, jnp.where(den_slot < 2 * PER, al, jnp.where(den_slot < 3 * PER, bh, bl)))
                den = jnp.where(den_live, den, 0.0).astype(BF)
                lhs = jnp.concatenate([a16 * m for m in masks] + [b16 * m for m in masks] + [den], axis=0)
                res = dot(lhs, qt[tile, rs])
                tail = jnp.broadcast_to(tails[c], (LANE, chunk))
                numer = numt[tile, rs] + jnp.where(tail, res[LANE : 2 * LANE], res[:LANE])
                d_all = res[2 * LANE :]
                d_a = d_all[0:PER] + d_all[PER : 2 * PER]
                d_b = d_all[2 * PER : 3 * PER] + d_all[3 * PER :]
                d_loc = dent[j, t * PER : (t + 1) * PER, rs]
                inv = 1.0 / (1.0 + d_loc + jnp.where(tail[:PER], d_b, d_a))
                scaled = [numer[i * HDIM : (i + 1) * HDIM] * inv[i : i + 1] for i in range(PER)]
                packs[c].append(jnp.concatenate(scaled, axis=0).astype(BF))
        cols = pl.ds(pl.multiple_of(j * BLK, BLK), BLK)
        for c in range(2):
            att[c * chunk : (c + 1) * chunk, cols] = jnp.transpose(jnp.concatenate(packs[c], axis=0))
        return carry_in

    lax.fori_loop(0, groups, combine, 0)

    ocopy.wait()
    square = jnp.zeros((toks, LANE), F32)

    def rise(b):
        end = min(b + BLK, d)
        if d - b > BLK:
            return dot(att[...], wo[:, b:end])
        return jnp.concatenate([dot(att[:chunk, :], wo[:, b:end]), dot(att[chunk:, :], wo[:, b:end])], axis=0)

    def settle(b, part_sum, square):
        end = min(b + BLK, d)
        mixed = hid[:, b:end].astype(F32) + part_sum
        sq = mixed * mixed
        for x in range(0, end - b, LANE):
            width = min(LANE, end - b - x)
            piece = sq[:, x : x + width]
            if width < LANE:
                piece = jnp.concatenate([piece, jnp.zeros((toks, LANE - width), F32)], axis=1)
            square = square + piece
        ybuf[:, b:end] = (mixed * jnp.broadcast_to(gain[b:end][None, :], mixed.shape)).astype(BF)
        return square

    for b in range(0, d, BLK):
        square = settle(b, rise(b), square)
    vel[...] = dot(ybuf[...], vwt[...])
    meansq = jnp.sum(square, axis=1, keepdims=True) * (1.0 / d)
    step = vel[...] * (0.5 * lax.rsqrt(meansq + 1e-06))
    lat = noisy[...] - jnp.transpose(step)
    lat_out[...] = lat
    xlat[0:HDIM, :] = lat

    outgoing[...] = dot_nt(onehot[...], xlat[...].astype(BF)).astype(BF)

    def out_copy(k):
        to = lax.rem(me + k, n)
        return remote(
            outgoing.at[pl.ds(pl.multiple_of(to * share, share), share)],
            incoming.at[pl.ds(pl.multiple_of(me * share, share), share)],
            asend.at[k], arecv.at[me], to,
        )

    for k in range(1, n):
        out_copy(k).start()
    own = pl.ds(pl.multiple_of(me * share, share), share)
    incoming[own, :] = outgoing[own, :]
    for k in range(1, n):
        src = lax.rem(me + k, n)
        remote(
            outgoing.at[pl.ds(0, share)],
            incoming.at[pl.ds(pl.multiple_of(src * share, share), share)],
            asend.at[k], arecv.at[src], src,
        ).wait_recv()

    got = incoming[...]
    lane_no = iota((8, 128), 1)
    pick = jnp.where(lane_no == HDIM, 1.0, jnp.where(lane_no == HDIM + 1, float(IW), 0.0)).astype(BF)
    pos = dot_nt(pick, got)[0:1, :].astype(jnp.int32)
    onehot[...] = (iota((toks, toks), 0) == jnp.broadcast_to(pos, (toks, toks))).astype(F32).astype(BF)
    tile = dot(onehot[...], got)
    edge = 2 * IW
    wide[edge : edge + toks, :] = tile
    halo_send[0] = tile[:edge].astype(BF)
    halo_send[1] = tile[toks - edge :].astype(BF)

    def halo(k, to):
        return remote(halo_send.at[k], halo_recv.at[k], halo_ssem.at[k], halo_rsem.at[k], to)

    @pl.when(me > 0)
    def _():
        halo(0, me - 1).start()

    @pl.when(me < n - 1)
    def _():
        halo(1, me + 1).start()

    wide[0:edge, :] = jnp.zeros((edge, 128), F32)
    wide[edge + toks :, :] = jnp.zeros((edge, 128), F32)

    @pl.when(me > 0)
    def _():
        halo(1, me - 1).wait_recv()
        wide[0:edge, :] = halo_recv[1].astype(F32)

    @pl.when(me < n - 1)
    def _():
        halo(0, me + 1).wait_recv()
        wide[edge + toks :, :] = halo_recv[0].astype(F32)

    ext = toks + 2 * edge
    x = wide[...]
    column = lax.rem(iota((ext, 128), 0), IW)
    lane = iota((ext, 128), 1)
    left = jnp.where(column == 0, 0.0, pltpu.roll(x, 1, 0))
    right = jnp.where(column == IW - 1, 0.0, pltpu.roll(x, ext - 1, 0))
    three = jnp.where(
        lane < HDIM, left,
        jnp.where(lane < 2 * HDIM, pltpu.roll(x, HDIM, 1),
                  jnp.where(lane < 3 * HDIM, pltpu.roll(right, 2 * HDIM, 1), 0.0)),
    )
    three = three.astype(BF)
    mid = toks + 2 * IW
    k3 = 3 * HDIM
    acc = dot(three[0:mid, :k3], w1[0])
    acc = acc + dot(three[IW : IW + mid, :k3], w1[1])
    acc = acc + dot(three[2 * IW : 2 * IW + mid, :k3], w1[2])
    feat = acc / (1.0 + jnp.exp(-acc))
    row_at = iota((mid, 1), 0) // IW
    outside = ((row_at == 0) & (me == 0)) | ((row_at == mid // IW - 1) & (me == n - 1))
    feat = jnp.where(outside, 0.0, feat).astype(BF).astype(F32)
    column = lax.rem(iota((mid, 1), 0), IW)
    shifted[1] = feat.astype(BF)
    shifted[0] = jnp.where(column == 0, 0.0, pltpu.roll(feat, 1, 0)).astype(BF)
    shifted[2] = jnp.where(column == IW - 1, 0.0, pltpu.roll(feat, mid - 1, 0)).astype(BF)
    w2copy.wait()
    out = None
    for a in range(3):
        for b in range(3):
            piece = dot(shifted[b, a * IW : a * IW + toks, :], w2[3 * a + b])
            out = piece if out is None else out + piece
    dec_out[...] = out.astype(BF)

    for k in range(1, TEAM):
        part_copy(k).wait_send()
        fin_copy(k).wait_send()

    for k in range(2):

        @pl.when(me >= k + 1)
        def _(k=k):
            lead_copy(k).wait_send()

    for to in range(1, teams):

        @pl.when(team < to)
        def _(to=to):
            plane_copy(to).wait_send()

    for k in range(1, n):
        out_copy(k).wait_send()

    @pl.when(me > 0)
    def _():
        halo(0, me - 1).wait_send()

    @pl.when(me < n - 1)
    def _():
        halo(1, me + 1).wait_send()


def body(
    hidden_in, noisy_latents, span_ids, tile_map, qkv_weight, out_weight,
    norm_gain, velocity_weight, conv_first, conv_second,
):
    toks, d = hidden_in.shape
    inner = out_weight.shape[0]
    n = lax.axis_size("span")
    ch = conv_first.shape[3]
    chunk = toks // 2
    lo = inner // BLK
    koff = inner - lo * BLK
    kw = -(-(koff + inner) // BLK) * BLK
    tiles = kw // LANE
    units = -(-(tiles + 1) // TEAM) * TEAM
    part = units // TEAM
    teams = n // TEAM
    edge = 2 * IW
    mid = toks + 2 * IW
    blocks = -(-qkv_weight.shape[1] // BLK)
    vm, dma = pltpu.VMEM, pltpu.SemaphoreType.DMA
    any_, vmem = pl.BlockSpec(memory_space=pl.ANY), pl.BlockSpec(memory_space=pltpu.VMEM)
    maps = tile_map.shape[0]
    half = HDIM // 2
    scratch = [
        vm((HDIM, toks), F32), vm((1, toks), jnp.int32), vm((1, maps), jnp.int32),
        vm((d,), F32), vm((HDIM, d), BF), vm((3, 3 * HDIM, ch), BF),
        vm((d, toks), BF), vm((toks, d), BF), vm(qkv_weight.shape, BF), vm((kw, d), BF),
        vm((9, ch, ch), BF),
        vm((kw, toks), BF), vm((toks, kw), BF), vm((kw, toks), BF),
        vm((kw, toks), F32), vm((kw // BLK, 8, toks), F32), vm((2, chunk, chunk), BF),
        vm((toks, kw), BF), vm((toks, d), BF), vm((d, HDIM), BF), vm((toks, HDIM), F32),
        vm((tiles, HDIM, LANE), F32), vm((tiles, HDIM, LANE), F32),
        vm((2, half, LANE), F32), vm((2, half, LANE), F32),
        vm((units, HDIM, LANE), BF), vm((units, HDIM, LANE), BF), vm((2, units, HDIM, LANE), BF),
        vm((TEAM, part, HDIM, LANE), BF), vm((part, HDIM, LANE), BF), vm((teams, part, HDIM, LANE), BF),
        vm((TEAM, part, HDIM, LANE), BF), vm((TEAM, part, HDIM, LANE), BF),
        vm((part, HDIM, LANE), F32), vm((units, HDIM, LANE), F32), vm((units, HDIM, LANE), F32),
        vm((toks, toks), BF), vm((128, toks), F32),
        vm((toks, 128), BF), vm((toks, 128), BF),
        vm((toks + 2 * edge, 128), F32), vm((2, edge, 128), BF), vm((2, edge, 128), BF),
        vm((3, mid, ch), BF),
        dma((blocks,)), dma((3,)), dma((toks // LANE,)), dma((6,)), dma((TEAM,)), dma((TEAM,)), dma((teams,)), dma((teams,)),
        dma((TEAM,)), dma((TEAM,)),
        dma((2,)), dma((2,)), dma((n,)), dma((n,)), dma((2,)), dma((2,)),
    ]
    latents, decoded = pl.pallas_call(
        functools.partial(kernel, (n, toks, d, inner)),
        out_shape=(
            jax.ShapeDtypeStruct(noisy_latents.shape[::-1], F32),
            jax.ShapeDtypeStruct((toks, ch), BF),
        ),
        in_specs=[any_] * 10,
        out_specs=(vmem, vmem),
        scratch_shapes=scratch,
        compiler_params=pltpu.CompilerParams(
            collective_id=0, has_side_effects=True, vmem_limit_bytes=60 * 1024 * 1024
        ),
    )(
        hidden_in.T, noisy_latents.T, span_ids.reshape(1, toks), tile_map.reshape(1, -1),
        qkv_weight, out_weight, norm_gain, velocity_weight.T,
        conv_first.reshape(3, 3 * HDIM, ch), conv_second.reshape(9, ch, ch),
    )
    return latents.T, decoded.reshape(toks // IW, IW, ch)


def solution(mesh):
    rows = P(("groups", "span"), None)
    placed = (rows, rows, P(("groups", "span")), P("groups")) + (P(),) * 6
    return jax.shard_map(
        body, mesh=mesh, in_specs=placed,
        out_specs=(rows, P(("groups", "span"), None, None)), check_vma=False,
    )
```

time: 58.7 us -> 51.6 us (0.88)
  Pallas kernels: 54.7 us -> 47.6 us
    pallas_call x1, Pallas kernels: 54.7 us -> 47.6 us  [body(): pl.pallas_call(functools.partial(kernel, (n, toks, d, inner)), out_shape=...]
where the time goes in v1:
time: 51.6 us; the launch traced here: 51.4 us
  Pallas kernels  47.6 us (92%)
  local copies, waits for them, and re-layouts  3.14 us (6%)
  between operations  0.64 us (1%)
    pallas_call x1, Pallas kernels, body(): pl.pallas_call(functools.partial(kernel, (n, toks, d, inner)), out_shape=...  47.6 us
    unnamed x2, local copies, waits for them, and re-layouts  3.14 us

profile of v1, /device:TPU:1, one launch (start us, length us, event | category | flops | bytes accessed | tf_op | source)
XLA Modules:
  0.0 51.4 jit_solution(18103304124743519001)
XLA Ops:
  0.6 47.6 %shard_map.113 = (f32[32,512]{1,0:T(8,128)}, bf16[512,256]{1,0:T(8,128)(2,1)}) custom-call(bf16[2240,512]{1,0:T(8,128)(2,1)} %bitcast.9, f32[32,512]{1,0:T(8,128)} %bitcast.14, s32[1,512]{1,0:T(1,128)} %bitcast.17, s32[1,8192]{1,0:T(1,128)} %bitcast.16, bf16[2240,3360]{1,0:T(8,128)(2,1)} %wq_hbm.1, bf16[1120,2240]{1,0:T(8,128)(2,1)} %wo_hbm.1, ...), custom_call_target="tpu_custom_call" | custom-call | tf_op jit(solution)/shard_map/pallas_call | solution.py:645
  48.3 1.5 %copy.14 = f32[512,32]{0,1:T(8,128)} copy(f32[512,32]{0,1:T(8,128)} %bitcast.15) | data formatting | bytes 131072
  49.7 1.7 %copy.15 = bf16[8,64,256]{2,1,0:T(8,128)(2,1)} copy(bf16[8,64,256]{2,1,0:T(8,128)(2,1)} %bitcast.11) | data formatting | bytes 524288

commit v2 on v1

--- a/solution.py
+++ b/solution.py
@@ -36,11 +36,11 @@
     hid_hbm, noisy_hbm, span_hbm, map_hbm, wq_hbm, wo_hbm, gain_hbm, vw_hbm, w1_hbm, w2_hbm,
     lat_out, dec_out,
     noisy, span_ref, map_ref, gain, vw, w1,
-    hidt, hid, wq, wo, w2, qt, kp, vt, numt, dent, keep, att, ybuf, vwt, vel,
+    hidt, hid, wq, wo, w2, qt, kp, vt, numt, dent, keep, att, ybuf, vwt,
     st_c0, st_b0, sum_c0, sum_b0, st_send, lead_send, lead_recv,
-    part_recv, plane_send, plane_recv, fin_send, fin_recv, base, carry, after, onehot, xlat, outgoing, incoming,
-    wide, halo_send, halo_recv, shifted,
-    wsem, lsem, hsem, isem, psend, precv, gsend, grecv, fsend, frecv, lead_ssem, lead_rsem, asend, arecv, halo_ssem, halo_rsem,
+    part_recv, plane_send, plane_recv, fin_send, fin_recv, base, carry, after, onehot, map_rows, place, noisy_t, outgoing, incoming,
+    wide, shifted,
+    wsem, lsem, hsem, isem, psend, precv, gsend, grecv, fsend, frecv, lead_ssem, lead_rsem, asend, arecv,
 ):
     n, toks, d, inner = cfg
     me = lax.axis_index("span")
@@ -48,6 +48,7 @@
     team = me // TEAM
     teams = n // TEAM
     share = toks // n
+    rows_to = share // PER
     chunk = toks // 2
     lo = inner // BLK
     koff = inner - lo * BLK
@@ -129,7 +130,7 @@
         rs = slice(c * chunk, (c + 1) * chunk)
         sr = span_row[:, rs]
         keep[c] = ((span_col[rs, :] <= sr) & (sr < lasts[c])).astype(F32).astype(BF)
-    vwt[...] = jnp.transpose(vw[...])
+    vwt[...] = jnp.concatenate([jnp.transpose(vw[...]), jnp.zeros((d, LANE - HDIM), F32).astype(BF)], axis=1)
 
     def turn(i, c):
         cols = pl.ds(pl.multiple_of(i * LANE, LANE), LANE)
@@ -250,27 +251,60 @@
             lax.rem(me - 1 - k + n, n),
         )
 
-    for k in range(2):
-
-        @pl.when(me >= k + 1)
-        def _(k=k):
-            lead_copy(k).start()
-
     mine = map_ref[:, pl.ds(pl.multiple_of(me * toks, toks), toks)]
     target = mine // toks
-    within = mine - target * toks
-    hits = (iota((n, toks), 0) == jnp.broadcast_to(target, (n, toks))).astype(F32)
+    for b in range(n):
+        map_rows[b : b + 1, :] = map_ref[:, b * toks : (b + 1) * toks]
+    goal = map_rows[...] // toks
+    where_in = map_rows[...] - goal * toks
+    hits = [iota((n, toks), 0) == jnp.broadcast_to(target, (n, toks))]
+    hits += [goal == me - 1 + x for x in range(3)]
     upper = (iota((toks, toks), 0) <= iota((toks, toks), 1)).astype(BF)
-    cum = dot(hits.astype(BF), upper)
-    rank = jnp.sum(cum * hits, axis=0, keepdims=True).astype(jnp.int32) - 1
-    slot = target * share + rank
+    cum = dot(jnp.concatenate([h.astype(F32) for h in hits], axis=0).astype(BF), upper)
+    rank = jnp.sum(jnp.where(hits[0], cum[:n], 0.0), axis=0, keepdims=True).astype(jnp.int32) - 1
+    packed = n * rows_to
+    slot = rank // rows_to * packed + target * rows_to + lax.rem(rank, rows_to)
     onehot[...] = (iota((toks, toks), 0) == jnp.broadcast_to(slot, (toks, toks))).astype(F32).astype(BF)
-    line = (within // IW).astype(F32)
-    spot = (within - within // IW * IW).astype(F32)
-    row_at = iota((128, toks), 0)
-    places = jnp.where(row_at == HDIM, jnp.broadcast_to(spot, (128, toks)), 0.0)
-    places = jnp.where(row_at == HDIM + 1, jnp.broadcast_to(line, (128, toks)), places)
-    xlat[...] = places
+    spot_f = where_in.astype(F32)
+    lane_n = iota((n, LANE), 1)
+    found = []
+    for x in range(3):
+        order = jnp.where(hits[1 + x], cum[n * (1 + x) : n * (2 + x)], 0.0)
+        table = jnp.zeros((n, LANE), F32)
+        for r in range(share):
+            one = jnp.sum(jnp.where(order == float(r + 1), spot_f, 0.0), axis=1, keepdims=True)
+            table = jnp.where(lane_n == r, one, table)
+        whole_pos = table.astype(jnp.int32)
+        found.append((whole_pos // IW).astype(F32))
+        found.append(lax.rem(whole_pos, IW).astype(F32))
+    slot_no = iota((LANE, toks), 1)
+    rank_of = slot_no // packed * rows_to + lax.rem(slot_no, rows_to)
+    spread = (iota((LANE, toks), 0) == rank_of).astype(F32).astype(BF)
+    filled = dot(jnp.concatenate(found, axis=0).astype(BF), spread)
+    source = lax.rem(iota((n, toks), 1), packed) // rows_to
+    owned = iota((n, toks), 0) == source
+    edge = 2 * IW
+    starts = (0, edge, edge + toks)
+    sizes = (edge, toks, edge)
+    for x in range(3):
+        lines, spots = [
+            jnp.sum(jnp.where(owned, filled[n * (2 * x + y) : n * (2 * x + y + 1)], 0.0), axis=0, keepdims=True)
+            for y in range(2)
+        ]
+        pos = (lines * float(IW) + spots).astype(jnp.int32)
+        if x == 0:
+            pos = pos - (toks - edge)
+        place[starts[x] : starts[x] + sizes[x], :] = (
+            iota((sizes[x], toks), 0) == jnp.broadcast_to(pos, (sizes[x], toks))
+        ).astype(F32).astype(BF)
+    for x in (0, n + 1):
+        outgoing[x] = jnp.zeros((rows_to, LANE), F32).astype(BF)
+    noisy_t[...] = jnp.concatenate(
+        [jnp.transpose(noisy[...]), jnp.zeros((toks, LANE - HDIM), F32)], axis=1
+    )
+
+    fetch(len(pending))
+    project(list(range(lo // 2)))
 
     part_recv[mate] = st_send[pl.ds(part * mate, part)]
     for k in range(1, TEAM):
@@ -288,14 +322,19 @@
             plane_send, plane_recv.at[team], gsend.at[to], grecv.at[team], TEAM * to + mate
         )
 
-    for to in range(1, teams):
+    for to in range(teams - 1, 0, -1):
 
         @pl.when(team < to)
         def _(to=to):
             plane_copy(to).start()
 
-    fetch(len(pending))
-    project(list(range(lo)))
+    for k in range(2):
+
+        @pl.when(me >= k + 1)
+        def _(k=k):
+            lead_copy(k).start()
+
+    project(list(range(lo // 2, lo)))
 
     def attend(jobs):
         def place(j, s):
@@ -348,7 +387,7 @@
         attend([(j, s, c) for s in range(slots_of) for c in range(2)])
         return carry_in
 
-    lax.fori_loop(plain[0], plain[-1] + 1, attend_loop, 0)
+    lax.fori_loop(plain[0], plain[-1], attend_loop, 0)
 
     base[...] = jnp.zeros_like(base)
     for src in range(teams - 1):
@@ -374,6 +413,8 @@
 
     for k in range(1, TEAM):
         fin_copy(k).start()
+
+    lax.fori_loop(plain[-1], plain[-1] + 1, attend_loop, 0)
 
     after[...] = jnp.zeros_like(after)
     for k in range(2):
@@ -472,69 +513,41 @@
 
     for b in range(0, d, BLK):
         square = settle(b, rise(b), square)
-    vel[...] = dot(ybuf[...], vwt[...])
+    vel = dot(ybuf[...], vwt[...])
     meansq = jnp.sum(square, axis=1, keepdims=True) * (1.0 / d)
-    step = vel[...] * (0.5 * lax.rsqrt(meansq + 1e-06))
-    lat = noisy[...] - jnp.transpose(step)
-    lat_out[...] = lat
-    xlat[0:HDIM, :] = lat
-
-    outgoing[...] = dot_nt(onehot[...], xlat[...].astype(BF)).astype(BF)
+    lat = noisy_t[...] - vel * (0.5 * lax.rsqrt(meansq + 1e-06))
+    noisy_t[...] = lat
+    sorted_lat = dot(onehot[...], lat.astype(BF))
+    dense = sorted_lat[:packed]
+    for a in range(1, PER):
+        dense = dense + pltpu.roll(sorted_lat[a * packed : (a + 1) * packed], a * HDIM, 1)
+    outgoing[1 : n + 1] = dense.reshape(n, rows_to, LANE).astype(BF)
+
+    def flip(k):
+        to, bit = 0, 1
+        while bit < n:
+            have = lax.rem(me // bit, 2)
+            to = to + bit * (1 - have if k & bit else have)
+            bit *= 2
+        return to
 
     def out_copy(k):
-        to = lax.rem(me + k, n)
-        return remote(
-            outgoing.at[pl.ds(pl.multiple_of(to * share, share), share)],
-            incoming.at[pl.ds(pl.multiple_of(me * share, share), share)],
-            asend.at[k], arecv.at[me], to,
-        )
-
+        to = flip(k)
+        return remote(outgoing.at[pl.ds(to, 3)], incoming.at[me], asend.at[k], arecv.at[me], to)
+
+    for k in range(n - 1, 0, -1):
+        out_copy(k).start()
+    incoming[me] = outgoing[pl.ds(me, 3)]
+    lat_out[...] = jnp.transpose(noisy_t[...])[:HDIM]
     for k in range(1, n):
-        out_copy(k).start()
-    own = pl.ds(pl.multiple_of(me * share, share), share)
-    incoming[own, :] = outgoing[own, :]
-    for k in range(1, n):
-        src = lax.rem(me + k, n)
-        remote(
-            outgoing.at[pl.ds(0, share)],
-            incoming.at[pl.ds(pl.multiple_of(src * share, share), share)],
-            asend.at[k], arecv.at[src], src,
-        ).wait_recv()
-
-    got = incoming[...]
-    lane_no = iota((8, 128), 1)
-    pick = jnp.where(lane_no == HDIM, 1.0, jnp.where(lane_no == HDIM + 1, float(IW), 0.0)).astype(BF)
-    pos = dot_nt(pick, got)[0:1, :].astype(jnp.int32)
-    onehot[...] = (iota((toks, toks), 0) == jnp.broadcast_to(pos, (toks, toks))).astype(F32).astype(BF)
-    tile = dot(onehot[...], got)
-    edge = 2 * IW
-    wide[edge : edge + toks, :] = tile
-    halo_send[0] = tile[:edge].astype(BF)
-    halo_send[1] = tile[toks - edge :].astype(BF)
-
-    def halo(k, to):
-        return remote(halo_send.at[k], halo_recv.at[k], halo_ssem.at[k], halo_rsem.at[k], to)
-
-    @pl.when(me > 0)
-    def _():
-        halo(0, me - 1).start()
-
-    @pl.when(me < n - 1)
-    def _():
-        halo(1, me + 1).start()
-
-    wide[0:edge, :] = jnp.zeros((edge, 128), F32)
-    wide[edge + toks :, :] = jnp.zeros((edge, 128), F32)
-
-    @pl.when(me > 0)
-    def _():
-        halo(1, me - 1).wait_recv()
-        wide[0:edge, :] = halo_recv[1].astype(F32)
-
-    @pl.when(me < n - 1)
-    def _():
-        halo(0, me + 1).wait_recv()
-        wide[edge + toks :, :] = halo_recv[0].astype(F32)
+        src = flip(k)
+        remote(outgoing.at[pl.ds(0, 3)], incoming.at[src], asend.at[k], arecv.at[src], src).wait_recv()
+
+    for x in range(3):
+        dense = incoming[:, x].astype(F32).reshape(packed, LANE)
+        slots = [dense] + [pltpu.roll(dense, LANE - a * HDIM, 1) for a in range(1, PER)]
+        at = slice(starts[x], starts[x] + sizes[x])
+        wide[at, :] = dot(place[at, :], jnp.concatenate(slots, axis=0).astype(BF))
 
     ext = toks + 2 * edge
     x = wide[...]
@@ -588,13 +601,16 @@
     for k in range(1, n):
         out_copy(k).wait_send()
 
-    @pl.when(me > 0)
-    def _():
-        halo(0, me - 1).wait_send()
-
-    @pl.when(me < n - 1)
-    def _():
-        halo(1, me + 1).wait_send()
+
+def flush(lat, dec, lat_out, dec_out, sem):
+    copies = [
+        pltpu.make_async_copy(dec, dec_out, sem.at[0]),
+        pltpu.make_async_copy(lat, lat_out, sem.at[1]),
+    ]
+    for copy in copies:
+        copy.start()
+    for copy in copies:
+        copy.wait()
 
 
 def body(
@@ -620,6 +636,7 @@
     any_, vmem = pl.BlockSpec(memory_space=pl.ANY), pl.BlockSpec(memory_space=pltpu.VMEM)
     maps = tile_map.shape[0]
     half = HDIM // 2
+    rows_to = toks // n // PER
     scratch = [
         vm((HDIM, toks), F32), vm((1, toks), jnp.int32), vm((1, maps), jnp.int32),
         vm((d,), F32), vm((HDIM, d), BF), vm((3, 3 * HDIM, ch), BF),
@@ -627,26 +644,26 @@
         vm((9, ch, ch), BF),
         vm((kw, toks), BF), vm((toks, kw), BF), vm((kw, toks), BF),
         vm((kw, toks), F32), vm((kw // BLK, 8, toks), F32), vm((2, chunk, chunk), BF),
-        vm((toks, kw), BF), vm((toks, d), BF), vm((d, HDIM), BF), vm((toks, HDIM), F32),
+        vm((toks, kw), BF), vm((toks, d), BF), vm((d, LANE), BF),
         vm((tiles, HDIM, LANE), F32), vm((tiles, HDIM, LANE), F32),
         vm((2, half, LANE), F32), vm((2, half, LANE), F32),
         vm((units, HDIM, LANE), BF), vm((units, HDIM, LANE), BF), vm((2, units, HDIM, LANE), BF),
         vm((TEAM, part, HDIM, LANE), BF), vm((part, HDIM, LANE), BF), vm((teams, part, HDIM, LANE), BF),
         vm((TEAM, part, HDIM, LANE), BF), vm((TEAM, part, HDIM, LANE), BF),
         vm((part, HDIM, LANE), F32), vm((units, HDIM, LANE), F32), vm((units, HDIM, LANE), F32),
-        vm((toks, toks), BF), vm((128, toks), F32),
-        vm((toks, 128), BF), vm((toks, 128), BF),
-        vm((toks + 2 * edge, 128), F32), vm((2, edge, 128), BF), vm((2, edge, 128), BF),
+        vm((toks, toks), BF), vm((n, toks), jnp.int32), vm((toks + 2 * edge, toks), BF), vm((toks, LANE), F32),
+        vm((n + 2, rows_to, LANE), BF), vm((n, 3, rows_to, LANE), BF),
+        vm((toks + 2 * edge, 128), F32),
         vm((3, mid, ch), BF),
         dma((blocks,)), dma((3,)), dma((toks // LANE,)), dma((6,)), dma((TEAM,)), dma((TEAM,)), dma((teams,)), dma((teams,)),
         dma((TEAM,)), dma((TEAM,)),
-        dma((2,)), dma((2,)), dma((n,)), dma((n,)), dma((2,)), dma((2,)),
+        dma((2,)), dma((2,)), dma((n,)), dma((n,)),
     ]
     latents, decoded = pl.pallas_call(
         functools.partial(kernel, (n, toks, d, inner)),
         out_shape=(
-            jax.ShapeDtypeStruct(noisy_latents.shape[::-1], F32),
-            jax.ShapeDtypeStruct((toks, ch), BF),
+            pltpu.VMEM(noisy_latents.shape[::-1], F32),
+            pltpu.VMEM((toks, ch), BF),
         ),
         in_specs=[any_] * 10,
         out_specs=(vmem, vmem),
@@ -659,6 +676,17 @@
         qkv_weight, out_weight, norm_gain, velocity_weight.T,
         conv_first.reshape(3, 3 * HDIM, ch), conv_second.reshape(9, ch, ch),
     )
+    latents, decoded = [pltpu.with_memory_space_constraint(x, pltpu.VMEM) for x in (latents, decoded)]
+    latents, decoded = pl.pallas_call(
+        flush,
+        out_shape=(
+            jax.ShapeDtypeStruct(latents.shape, F32),
+            jax.ShapeDtypeStruct(decoded.shape, BF),
+        ),
+        in_specs=[vmem, vmem],
+        out_specs=(any_, any_),
+        scratch_shapes=[dma((2,))],
+    )(latents, decoded)
     return latents.T, decoded.reshape(toks // IW, IW, ch)
 
 

time: 51.6 us -> 42.5 us (0.82)
  the two profiles are of different devices: /device:TPU:1 before, /device:TPU:0 now
where the time goes in v2:
time: 42.5 us; the launch traced here: 42.4 us
  Pallas kernels  41.5 us (98%)
  between operations  0.8 us (2%)
    pallas_call x1, Pallas kernels, body(): pl.pallas_call(functools.partial(kernel, (n, toks, d, inner)), out_shape=...  40.8 us

profile of v2, /device:TPU:0, one launch (start us, length us, event | category | flops | bytes accessed | tf_op | source)
XLA Modules:
  0.0 42.4 jit_solution(6108913178776760366)
XLA Ops:
  0.6 40.8 %shard_map.113 = (f32[32,512]{1,0:T(8,128)S(1)}, bf16[512,256]{1,0:T(8,128)(2,1)S(1)}) custom-call(bf16[2240,512]{1,0:T(8,128)(2,1)} %bitcast.9, f32[32,512]{1,0:T(8,128)} %bitcast.13, s32[1,512]{1,0:T(1,128)} %bitcast.15, s32[1,8192]{1,0:T(1,128)} %bitcast.14, bf16[2240,3360]{1,0:T(8,128)(2,1)} %wq_hbm.1, bf16[1120,2240]{1,0:T(8,128)(2,1)} %wo_hbm.1, ...), custom_call_target="tpu_custom_call" | custom-call | tf_op jit(solution)/shard_map/pallas_call | solution.py:662
  41.5 0.7 %shard_map.114 = (f32[32,512]{1,0:T(8,128)}, bf16[512,256]{1,0:T(8,128)(2,1)}) custom-call(f32[32,512]{1,0:T(8,128)S(1)} %get-tuple-element.6.lat, bf16[512,256]{1,0:T(8,128)(2,1)S(1)} %get-tuple-element.7.dec), custom_call_target="tpu_custom_call" | custom-call | tf_op jit(solution)/shard_map/pallas_call | solution.py:680

commit v3 on v2

--- a/solution.py
+++ b/solution.py
@@ -37,7 +37,7 @@
     lat_out, dec_out,
     noisy, span_ref, map_ref, gain, vw, w1,
     hidt, hid, wq, wo, w2, qt, kp, vt, numt, dent, keep, att, ybuf, vwt,
-    st_c0, st_b0, sum_c0, sum_b0, st_send, lead_send, lead_recv,
+    st_c0, st_b0, st_all, st_lead, sum_c0, sum_b0, st_send, lead_send, lead_recv,
     part_recv, plane_send, plane_recv, fin_send, fin_recv, base, carry, after, onehot, map_rows, place, noisy_t, outgoing, incoming,
     wide, shifted,
     wsem, lsem, hsem, isem, psend, precv, gsend, grecv, fsend, frecv, lead_ssem, lead_rsem, asend, arecv,
@@ -54,8 +54,9 @@
     koff = inner - lo * BLK
     kw = kp.shape[1]
     tiles = kw // LANE
-    units = st_send.shape[0]
-    part = units // TEAM
+    units = st_send.shape[0] // 2
+    part = 2 * units // TEAM
+    half = HDIM // 2
     heads = inner // HDIM
     first_slot = koff // HDIM
     last_slot = first_slot + heads
@@ -209,8 +210,8 @@
             s0 = diag(c0, t)
             st_c0[u] = s0
             st_b0[u] = s0 + diag(b0, t)
-            st_send[u] = (s0 + diag(c1, t)).astype(BF)
-            lead_send[u] = (diag(l0, t) + diag(l1, t)).astype(BF)
+            st_all[u] = s0 + diag(c1, t)
+            st_lead[u] = diag(l0, t) + diag(l1, t)
             at = slice(t * LANE, (t + 1) * LANE)
             one = slice(BLK, BLK + 1)
             sum_c0[0, u : u + 1, :] = c0[one, at]
@@ -218,20 +219,25 @@
             sum_c0[1, u : u + 1, :] = c0[one, at] + c1[one, at]
             sum_b0[1, u : u + 1, :] = l0[one, at] + l1[one, at]
 
-    half = HDIM // 2
     row_no = iota((half, LANE), 0)
-
-    def pack_sums(dst, sums):
+    last_tile = tiles - 1
+
+    def pack(dst, src, sums):
+        for u in range(last_tile):
+            full_unit = src[u] + src[last_tile] if u == 0 else src[u]
+            for x in range(2):
+                dst[2 * u + x] = full_unit[x * half : (x + 1) * half].astype(BF)
         sums = jnp.where(row_no < tiles, sums, 0.0)
         high = sums.astype(BF).astype(F32)
         low = sums - high
         high = jnp.where(row_no == half - 1, jnp.broadcast_to(first_seg, (half, LANE)), high)
-        dst[tiles] = jnp.concatenate([high, low], axis=0).astype(BF)
-        for u in range(tiles + 1, units):
-            dst[u] = jnp.zeros((HDIM, LANE), F32).astype(BF)
-
-    pack_sums(st_send, sum_c0[1])
-    pack_sums(lead_send, sum_b0[1])
+        dst[2 * last_tile] = high.astype(BF)
+        dst[2 * last_tile + 1] = low.astype(BF)
+        for u in range(2 * tiles, 2 * units):
+            dst[u] = jnp.zeros((half, LANE), F32).astype(BF)
+
+    pack(st_send, st_all, sum_c0[1])
+    pack(lead_send, st_lead, sum_b0[1])
 
     pl.semaphore_wait(barrier, n - 1)
 
@@ -416,6 +422,54 @@
 
     lax.fori_loop(plain[-1], plain[-1] + 1, attend_loop, 0)
 
+    tails = [span_row[:, c * chunk : (c + 1) * chunk] == lasts[c] for c in range(2)]
+    masks = [(lane_slot == i).astype(F32).astype(BF) for i in range(PER)]
+    den_slot = iota((half, LANE), 0)
+    den_live = lax.rem(den_slot, PER) == iota((half, LANE), 1) // HDIM
+
+    def left_side(states, sums):
+        rows = []
+        for state in states:
+            state = state.astype(BF)
+            rows += [state * m for m in masks]
+        levels = []
+        for total_sum in sums:
+            high = total_sum.astype(BF).astype(F32)
+            levels += [high, total_sum - high]
+        den = jnp.broadcast_to(levels[-1], (half, LANE))
+        for x in range(len(levels) - 2, -1, -1):
+            den = jnp.where(den_slot < PER * (x + 1), levels[x], den)
+        live = den_live & (den_slot < PER * len(levels))
+        return jnp.concatenate(rows + [jnp.where(live, den, 0.0).astype(BF)], axis=0)
+
+    def inside(j, carry_in):
+        work = []
+        for t in range(2):
+            u = 2 * j + t
+            tile = pl.ds(pl.multiple_of(j * BLK + t * LANE, LANE), LANE)
+            one = pl.ds(u, 1)
+            lhs = [
+                left_side([st_b0[u]], [sum_b0[0, one, :]]),
+                left_side([st_c0[u], st_all[u]], [sum_c0[0, one, :], sum_c0[1, one, :]]),
+            ]
+            for c in range(2):
+                rs = slice(c * chunk, (c + 1) * chunk)
+                work.append((t, c, tile, rs, dot(lhs[c], qt[tile, rs])))
+        for t, c, tile, rs, res in work:
+            tail = jnp.broadcast_to(tails[c], (LANE, chunk))
+            d_all = res[LANE * (c + 1) :]
+            d_one = d_all[:PER] + d_all[PER : 2 * PER]
+            if c == 0:
+                more, d_more = jnp.where(tail, res[:LANE], 0.0), jnp.where(tail[:PER], d_one, 0.0)
+            else:
+                d_two = d_all[2 * PER : 3 * PER] + d_all[3 * PER :]
+                more, d_more = jnp.where(tail, res[LANE : 2 * LANE], res[:LANE]), jnp.where(tail[:PER], d_two, d_one)
+            numt[tile, rs] = numt[tile, rs] + more
+            dent[j, t * PER : (t + 1) * PER, rs] = dent[j, t * PER : (t + 1) * PER, rs] + d_more
+        return carry_in
+
+    lax.fori_loop(0, groups, inside, 0)
+
     after[...] = jnp.zeros_like(after)
     for k in range(2):
 
@@ -424,7 +478,7 @@
             remote(
                 lead_send, lead_recv.at[k], lead_ssem.at[k], lead_rsem.at[k], lax.rem(me + 1 + k, n)
             ).wait_recv()
-            same = (lead_recv[k, tiles, half - 1 : half, 0:1].astype(F32) == last_seg).astype(F32)
+            same = (lead_recv[k, 2 * last_tile, half - 1 : half, 0:1].astype(F32) == last_seg).astype(F32)
             after[...] = after[...] + lead_recv[k].astype(F32) * same
 
     fin_recv[mate] = fin_send[mate]
@@ -436,58 +490,43 @@
     for m in range(TEAM):
         carry[m * part : (m + 1) * part] = fin_recv[m].astype(F32)
 
-    reach = [(lasts[c] == last_seg).astype(F32) for c in range(2)]
-    tails = [span_row[:, c * chunk : (c + 1) * chunk] == lasts[c] for c in range(2)]
-    masks = [(lane_slot == i).astype(F32).astype(BF) for i in range(PER)]
-    den_slot = iota((half, LANE), 0)
-    den_lane = iota((half, LANE), 1) // HDIM
-    den_live = lax.rem(den_slot, PER) == den_lane
+    reach_row = jnp.concatenate(
+        [(tails[c] & (lasts[c] == last_seg)).astype(F32) for c in range(2)], axis=1
+    )
+
+    def unit_of(ref, u):
+        u = 0 if u == last_tile else u
+        return jnp.concatenate([ref[2 * u], ref[2 * u + 1]], axis=0)
 
     def sums_of(ref, u):
-        return ref[tiles, pl.ds(u, 1), :] + ref[tiles, pl.ds(half + u, 1), :]
-
-    def combine(j, carry_in):
-        packs = [[], []]
+        return ref[2 * last_tile, u : u + 1, :] + ref[2 * last_tile + 1, u : u + 1, :]
+
+    def outside(j):
+        out = []
         for t in range(2):
             u = 2 * j + t
-            tile = pl.ds(pl.multiple_of(j * BLK + t * LANE, LANE), LANE)
-            car, aft = carry[u], after[u]
-            csum, asum = sums_of(carry, u), sums_of(after, u)
-            for c in range(2):
-                rs = slice(c * chunk, (c + 1) * chunk)
-                if c == 0:
-                    a_state, a_sum = car, csum
-                    b_state = st_b0[u] + car + aft * reach[0]
-                    b_sum = sum_b0[0, pl.ds(u, 1), :] + csum + asum * reach[0]
-                else:
-                    a_state, a_sum = st_c0[u] + car, sum_c0[0, pl.ds(u, 1), :] + csum
-                    b_state = st_send[u].astype(F32) + car + aft
-                    b_sum = sum_c0[1, pl.ds(u, 1), :] + csum + asum
-                a16, b16 = a_state.astype(BF), b_state.astype(BF)
-                dens = []
-                for s in (a_sum, b_sum):
-                    high = s.astype(BF).astype(F32)
-                    dens.append((high, s - high))
-                (ah, al), (bh, bl) = dens
-                den = jnp.where(den_slot < PER, ah, jnp.where(den_slot < 2 * PER, al, jnp.where(den_slot < 3 * PER, bh, bl)))
-                den = jnp.where(den_live, den, 0.0).astype(BF)
-                lhs = jnp.concatenate([a16 * m for m in masks] + [b16 * m for m in masks] + [den], axis=0)
-                res = dot(lhs, qt[tile, rs])
-                tail = jnp.broadcast_to(tails[c], (LANE, chunk))
-                numer = numt[tile, rs] + jnp.where(tail, res[LANE : 2 * LANE], res[:LANE])
-                d_all = res[2 * LANE :]
-                d_a = d_all[0:PER] + d_all[PER : 2 * PER]
-                d_b = d_all[2 * PER : 3 * PER] + d_all[3 * PER :]
-                d_loc = dent[j, t * PER : (t + 1) * PER, rs]
-                inv = 1.0 / (1.0 + d_loc + jnp.where(tail[:PER], d_b, d_a))
-                scaled = [numer[i * HDIM : (i + 1) * HDIM] * inv[i : i + 1] for i in range(PER)]
-                packs[c].append(jnp.concatenate(scaled, axis=0).astype(BF))
-        cols = pl.ds(pl.multiple_of(j * BLK, BLK), BLK)
-        for c in range(2):
-            att[c * chunk : (c + 1) * chunk, cols] = jnp.transpose(jnp.concatenate(packs[c], axis=0))
-        return carry_in
-
-    lax.fori_loop(0, groups, combine, 0)
+            lhs = left_side([unit_of(carry, u), unit_of(after, u)], [sums_of(carry, u), sums_of(after, u)])
+            out.append(dot(lhs, qt[u * LANE : (u + 1) * LANE, :]))
+        return out
+
+    def close(j, parts):
+        rows = []
+        for t, res in enumerate(parts):
+            u = 2 * j + t
+            reach = jnp.broadcast_to(reach_row, (LANE, toks))
+            numer = numt[u * LANE : (u + 1) * LANE, :] + res[:LANE] + reach * res[LANE : 2 * LANE]
+            d_all = res[2 * LANE :]
+            den = d_all[:PER] + d_all[PER : 2 * PER] + reach[:PER] * (d_all[2 * PER : 3 * PER] + d_all[3 * PER :])
+            inv = 1.0 / (1.0 + dent[j, t * PER : (t + 1) * PER, :] + den)
+            rows += [(numer[i * HDIM : (i + 1) * HDIM] * inv[i : i + 1]).astype(BF) for i in range(PER)]
+        att[:, j * BLK : (j + 1) * BLK] = jnp.transpose(jnp.concatenate(rows, axis=0))
+
+    held = outside(0)
+    for j in range(1, groups):
+        coming = outside(j)
+        close(j - 1, held)
+        held = coming
+    close(groups - 1, held)
 
     ocopy.wait()
     square = jnp.zeros((toks, LANE), F32)
@@ -626,8 +665,8 @@
     koff = inner - lo * BLK
     kw = -(-(koff + inner) // BLK) * BLK
     tiles = kw // LANE
-    units = -(-(tiles + 1) // TEAM) * TEAM
-    part = units // TEAM
+    units = -(-2 * tiles // TEAM) * TEAM // 2
+    part = 2 * units // TEAM
     teams = n // TEAM
     edge = 2 * IW
     mid = toks + 2 * IW
@@ -646,11 +685,12 @@
         vm((kw, toks), F32), vm((kw // BLK, 8, toks), F32), vm((2, chunk, chunk), BF),
         vm((toks, kw), BF), vm((toks, d), BF), vm((d, LANE), BF),
         vm((tiles, HDIM, LANE), F32), vm((tiles, HDIM, LANE), F32),
+        vm((tiles, HDIM, LANE), F32), vm((tiles, HDIM, LANE), F32),
         vm((2, half, LANE), F32), vm((2, half, LANE), F32),
-        vm((units, HDIM, LANE), BF), vm((units, HDIM, LANE), BF), vm((2, units, HDIM, LANE), BF),
-        vm((TEAM, part, HDIM, LANE), BF), vm((part, HDIM, LANE), BF), vm((teams, part, HDIM, LANE), BF),
-        vm((TEAM, part, HDIM, LANE), BF), vm((TEAM, part, HDIM, LANE), BF),
-        vm((part, HDIM, LANE), F32), vm((units, HDIM, LANE), F32), vm((units, HDIM, LANE), F32),
+        vm((2 * units, half, LANE), BF), vm((2 * units, half, LANE), BF), vm((2, 2 * units, half, LANE), BF),
+        vm((TEAM, part, half, LANE), BF), vm((part, half, LANE), BF), vm((teams, part, half, LANE), BF),
+        vm((TEAM, part, half, LANE), BF), vm((TEAM, part, half, LANE), BF),
+        vm((part, half, LANE), F32), vm((2 * units, half, LANE), F32), vm((2 * units, half, LANE), F32),
         vm((toks, toks), BF), vm((n, toks), jnp.int32), vm((toks + 2 * edge, toks), BF), vm((toks, LANE), F32),
         vm((n + 2, rows_to, LANE), BF), vm((n, 3, rows_to, LANE), BF),
         vm((toks + 2 * edge, 128), F32),

time: 42.5 us -> 41.1 us (0.967)
  the two profiles are of different devices: /device:TPU:0 before, /device:TPU:1 now
where the time goes in v3:
time: 41.1 us; the launch traced here: 40.3 us
  Pallas kernels  39.5 us (96%)
  between operations  0.8 us (2%)
    pallas_call x1, Pallas kernels, body(): pl.pallas_call(functools.partial(kernel, (n, toks, d, inner)), out_shape=...  38.7 us

profile of v3, /device:TPU:1, one launch (start us, length us, event | category | flops | bytes accessed | tf_op | source)
XLA Modules:
  0.0 40.3 jit_solution(7571608400107997526)
XLA Ops:
  0.6 38.7 %shard_map.113 = (f32[32,512]{1,0:T(8,128)S(1)}, bf16[512,256]{1,0:T(8,128)(2,1)S(1)}) custom-call(bf16[2240,512]{1,0:T(8,128)(2,1)} %bitcast.9, f32[32,512]{1,0:T(8,128)} %bitcast.13, s32[1,512]{1,0:T(1,128)} %bitcast.15, s32[1,8192]{1,0:T(1,128)} %bitcast.14, bf16[2240,3360]{1,0:T(8,128)(2,1)} %wq_hbm.1, bf16[1120,2240]{1,0:T(8,128)(2,1)} %wo_hbm.1, ...), custom_call_target="tpu_custom_call" | custom-call | tf_op jit(solution)/shard_map/pallas_call | solution.py:702
  39.4 0.7 %shard_map.114 = (f32[32,512]{1,0:T(8,128)}, bf16[512,256]{1,0:T(8,128)(2,1)}) custom-call(f32[32,512]{1,0:T(8,128)S(1)} %get-tuple-element.6.lat, bf16[512,256]{1,0:T(8,128)(2,1)S(1)} %get-tuple-element.7.dec), custom_call_target="tpu_custom_call" | custom-call | tf_op jit(solution)/shard_map/pallas_call | solution.py:720

commit v4 on v3

--- a/solution.py
+++ b/solution.py
@@ -139,14 +139,8 @@
         hid[cols, :] = jnp.transpose(hidt[:, cols])
         return c
 
-    lax.fori_loop(0, toks // LANE, turn, 0)
+    lax.fori_loop(0, chunk // LANE, turn, 0)
     fetch(2)
-
-    if rest:
-        wcopy(full).wait()
-        tail_w = jnp.transpose(wq[:, full * BLK : total])
-        row = full * BLK - 2 * inner + koff
-        vt[row : row + rest, :] = dot(tail_w, hidt[...]).astype(BF)
 
     def finish(out, b, rs):
         begin, end = b * BLK, b * BLK + BLK
@@ -165,19 +159,40 @@
             row = begin + skip - 2 * inner + koff
             vt[row : row + BLK - skip, rs] = jnp.transpose(out)[skip:]
 
-    def project(blocks):
-        for b in blocks:
-            wcopy(b).wait()
-        fetch(3)
+    def project(blocks, ready=False, spans=None):
+        if not ready:
+            for b in blocks:
+                wcopy(b).wait()
+            fetch(3)
         for at, b in enumerate(blocks):
             cols = slice(b * BLK, b * BLK + BLK)
             pair = len(blocks) % 2 == 1 and at == len(blocks) - 1
-            for rs in [slice(0, chunk), slice(chunk, toks)] if pair else [slice(0, toks)]:
+            for rs in spans or ([slice(0, chunk), slice(chunk, toks)] if pair else [slice(0, toks)]):
                 finish(dot(hid[rs, :], wq[:, cols]).astype(BF), b, rs)
+
+    def project_rest():
+        tail_w = jnp.transpose(wq[:, full * BLK : total])
+        row = full * BLK - 2 * inner + koff
+        vt[row : row + rest, :] = dot(tail_w, hidt[...]).astype(BF)
 
     early = list(range(lo, full))
     for at in range(0, len(early) - 1, 2):
-        project(early[at : at + (2 if at + 3 < len(early) else 3)])
+        blocks = early[at : at + (2 if at + 3 < len(early) else 3)]
+        if at > 0:
+            project(blocks)
+            continue
+        for b in blocks + ([full] if rest else []):
+            wcopy(b).wait()
+        for i in range(chunk // LANE, toks // LANE):
+            hcopy(i).wait()
+        fetch(3)
+        project(blocks, ready=True, spans=[slice(0, chunk)])
+        for i in range(chunk // LANE, toks // LANE):
+            rows = slice(i * LANE, (i + 1) * LANE)
+            hid[rows, :] = jnp.transpose(hidt[:, rows])
+        if rest:
+            project_rest()
+        project(blocks, ready=True, spans=[slice(chunk, toks)])
     for copy in smalls[2:]:
         copy.wait()
 
@@ -193,31 +208,22 @@
             out = jnp.where(lane_slot == i, parts[i], out)
         return out
 
+    at_tile = [slice(0, LANE), slice(LANE, BLK)]
+    one = slice(BLK, BLK + 1)
+
+    def sides(j, c):
+        cols, rs = slice(j * BLK, (j + 1) * BLK), slice(c * chunk, (c + 1) * chunk)
+        return jnp.concatenate([vt[cols, rs], ones16], axis=0), kp[rs, cols]
+
     for j in range(tiles // 2):
-        cols = slice(j * BLK, (j + 1) * BLK)
-        res = []
-        for c in range(2):
-            rs = slice(c * chunk, (c + 1) * chunk)
-            k8 = kp[rs, cols]
-            lhs = jnp.concatenate([vt[cols, rs], ones16], axis=0)
-            res.append(dot(lhs, k8))
-            res.append(dot(lhs * lead_row[:, rs], k8))
-            if c == 1:
-                res.append(dot(lhs * b0_row, k8))
-        c0, l0, c1, l1, b0 = res
+        c0, c1 = [dot(*sides(j, c)) for c in range(2)]
         for t in range(2):
             u = 2 * j + t
             s0 = diag(c0, t)
             st_c0[u] = s0
-            st_b0[u] = s0 + diag(b0, t)
             st_all[u] = s0 + diag(c1, t)
-            st_lead[u] = diag(l0, t) + diag(l1, t)
-            at = slice(t * LANE, (t + 1) * LANE)
-            one = slice(BLK, BLK + 1)
-            sum_c0[0, u : u + 1, :] = c0[one, at]
-            sum_b0[0, u : u + 1, :] = c0[one, at] + b0[one, at]
-            sum_c0[1, u : u + 1, :] = c0[one, at] + c1[one, at]
-            sum_b0[1, u : u + 1, :] = l0[one, at] + l1[one, at]
+            sum_c0[0, u : u + 1, :] = c0[one, at_tile[t]]
+            sum_c0[1, u : u + 1, :] = c0[one, at_tile[t]] + c1[one, at_tile[t]]
 
     row_no = iota((half, LANE), 0)
     last_tile = tiles - 1
@@ -237,7 +243,6 @@
             dst[u] = jnp.zeros((half, LANE), F32).astype(BF)
 
     pack(st_send, st_all, sum_c0[1])
-    pack(lead_send, st_lead, sum_b0[1])
 
     pl.semaphore_wait(barrier, n - 1)
 
@@ -257,6 +262,22 @@
             lax.rem(me - 1 - k + n, n),
         )
 
+    for j in range(tiles // 2):
+        (v0, k0), (v1, k1) = sides(j, 0), sides(j, 1)
+        l0, l1 = dot(v0 * lead_row[:, :chunk], k0), dot(v1 * lead_row[:, chunk:], k1)
+        b0 = dot(v1 * b0_row, k1)
+        for t in range(2):
+            u = 2 * j + t
+            st_b0[u] = st_c0[u] + diag(b0, t)
+            st_lead[u] = diag(l0, t) + diag(l1, t)
+            sum_b0[0, u : u + 1, :] = sum_c0[0, u : u + 1, :] + b0[one, at_tile[t]]
+            sum_b0[1, u : u + 1, :] = l0[one, at_tile[t]] + l1[one, at_tile[t]]
+
+    pack(lead_send, st_lead, sum_b0[1])
+
+    fetch(len(pending))
+    for b in range(lo // 2):
+        wcopy(b).wait()
     mine = map_ref[:, pl.ds(pl.multiple_of(me * toks, toks), toks)]
     target = mine // toks
     for b in range(n):
@@ -271,6 +292,7 @@
     packed = n * rows_to
     slot = rank // rows_to * packed + target * rows_to + lax.rem(rank, rows_to)
     onehot[...] = (iota((toks, toks), 0) == jnp.broadcast_to(slot, (toks, toks))).astype(F32).astype(BF)
+    project(list(range(lo // 2)), ready=True)
     spot_f = where_in.astype(F32)
     lane_n = iota((n, LANE), 1)
     found = []
@@ -308,9 +330,6 @@
     noisy_t[...] = jnp.concatenate(
         [jnp.transpose(noisy[...]), jnp.zeros((toks, LANE - HDIM), F32)], axis=1
     )
-
-    fetch(len(pending))
-    project(list(range(lo // 2)))
 
     part_recv[mate] = st_send[pl.ds(part * mate, part)]
     for k in range(1, TEAM):

time: 41.1 us -> 40 us (0.973)
  Pallas kernels: 39.5 us -> 38.5 us
    pallas_call x1, Pallas kernels: 38.7 us -> 37.7 us  [body(): pl.pallas_call(functools.partial(kernel, (n, toks, d, inner)), out_shape=...]
where the time goes in v4:
time: 40 us; the launch traced here: 39.3 us
  Pallas kernels  38.5 us (96%)
  between operations  0.8 us (2%)
    pallas_call x1, Pallas kernels, body(): pl.pallas_call(functools.partial(kernel, (n, toks, d, inner)), out_shape=...  37.7 us

profile of v4, /device:TPU:1, one launch (start us, length us, event | category | flops | bytes accessed | tf_op | source)
XLA Modules:
  0.0 39.3 jit_solution(14262219805109236759)
XLA Ops:
  0.6 37.7 %shard_map.113 = (f32[32,512]{1,0:T(8,128)S(1)}, bf16[512,256]{1,0:T(8,128)(2,1)S(1)}) custom-call(bf16[2240,512]{1,0:T(8,128)(2,1)} %bitcast.9, f32[32,512]{1,0:T(8,128)} %bitcast.13, s32[1,512]{1,0:T(1,128)} %bitcast.15, s32[1,8192]{1,0:T(1,128)} %bitcast.14, bf16[2240,3360]{1,0:T(8,128)(2,1)} %wq_hbm.1, bf16[1120,2240]{1,0:T(8,128)(2,1)} %wo_hbm.1, ...), custom_call_target="tpu_custom_call" | custom-call | tf_op jit(solution)/shard_map/pallas_call | solution.py:721
  38.4 0.7 %shard_map.114 = (f32[32,512]{1,0:T(8,128)}, bf16[512,256]{1,0:T(8,128)(2,1)}) custom-call(f32[32,512]{1,0:T(8,128)S(1)} %get-tuple-element.6.lat, bf16[512,256]{1,0:T(8,128)(2,1)S(1)} %get-tuple-element.7.dec), custom_call_target="tpu_custom_call" | custom-call | tf_op jit(solution)/shard_map/pallas_call | solution.py:739

commit v5 on v4

--- a/solution.py
+++ b/solution.py
@@ -569,9 +569,15 @@
         ybuf[:, b:end] = (mixed * jnp.broadcast_to(gain[b:end][None, :], mixed.shape)).astype(BF)
         return square
 
+    vel = jnp.zeros((toks, LANE), F32)
+    done = 0
     for b in range(0, d, BLK):
-        square = settle(b, rise(b), square)
-    vel = dot(ybuf[...], vwt[...])
+        part_sum = rise(b)
+        if b - done >= 4 * BLK:
+            vel = vel + dot(ybuf[:, done:b], vwt[done:b, :])
+            done = b
+        square = settle(b, part_sum, square)
+    vel = vel + dot(ybuf[:, done:], vwt[done:, :])
     meansq = jnp.sum(square, axis=1, keepdims=True) * (1.0 / d)
     lat = noisy_t[...] - vel * (0.5 * lax.rsqrt(meansq + 1e-06))
     noisy_t[...] = lat

time: 40 us -> 40 us (level)
  no operation moved by 1% of the time
where the time goes in v5:
time: 40 us; the launch traced here: 39.3 us
  Pallas kernels  38.5 us (96%)
  between operations  0.8 us (2%)
    pallas_call x1, Pallas kernels, body(): pl.pallas_call(functools.partial(kernel, (n, toks, d, inner)), out_shape=...  37.7 us

profile of v5, /device:TPU:1, one launch (start us, length us, event | category | flops | bytes accessed | tf_op | source)
XLA Modules:
  0.0 39.3 jit_solution(10391149505736580908)
XLA Ops:
  0.6 37.7 %shard_map.113 = (f32[32,512]{1,0:T(8,128)S(1)}, bf16[512,256]{1,0:T(8,128)(2,1)S(1)}) custom-call(bf16[2240,512]{1,0:T(8,128)(2,1)} %bitcast.9, f32[32,512]{1,0:T(8,128)} %bitcast.13, s32[1,512]{1,0:T(1,128)} %bitcast.15, s32[1,8192]{1,0:T(1,128)} %bitcast.14, bf16[2240,3360]{1,0:T(8,128)(2,1)} %wq_hbm.1, bf16[1120,2240]{1,0:T(8,128)(2,1)} %wo_hbm.1, ...), custom_call_target="tpu_custom_call" | custom-call | tf_op jit(solution)/shard_map/pallas_call | solution.py:727
  38.4 0.7 %shard_map.114 = (f32[32,512]{1,0:T(8,128)}, bf16[512,256]{1,0:T(8,128)(2,1)}) custom-call(f32[32,512]{1,0:T(8,128)S(1)} %get-tuple-element.6.lat, bf16[512,256]{1,0:T(8,128)(2,1)S(1)} %get-tuple-element.7.dec), custom_call_target="tpu_custom_call" | custom-call | tf_op jit(solution)/shard_map/pallas_call | solution.py:745
